TPU v7x, 512 devices: a whole 4x8x8 slice. The times are simulated.
512 devices in a mesh: grp: 32 (over z, x), vox: 16 (over y, core).
Axes of the slice: x: 4, y: 8, z: 8, core: 2. Of those that a mesh axis runs over, the one named last changes fastest.
Arguments:
- group_basis: bfloat16 [32, 16384, 256], P('grp', 'vox'), may hold values from -6 to 6
- timeseries: bfloat16 [32, 16384, 512], P('grp', 'vox'), may hold values from -6 to 6
Outputs:
- loadings: float32 [32, 256, 512], P('grp', 'vox')
All inputs are finite; a program needn't handle non-finite values.
Results may differ from a plain program's by a relative error of at most 0.015.
Values may be sent and summed in bfloat16 or wider, within the bound.
No kernel may reach another device: no remote copies, remote signals or barrier semaphores. Data moves between devices by JAX's collectives and lax.ppermute only.
A program may use at most 64 MiB of HBM per device.

v0:
```python
import functools

import jax
import jax.numpy as jnp
from jax import lax
from jax.experimental import pallas as pl
from jax.experimental.pallas import tpu as pltpu
from jax.sharding import PartitionSpec as P


N = 256
VOX = 16
GRP = 32
ROWS = N // VOX
F32 = jnp.float32
BF16 = jnp.bfloat16

NN = (((1,), (0,)), ((), ()))
NT = (((1,), (1,)), ((), ()))
TN = (((0,), (0,)), ((), ()))
VMEM = pl.BlockSpec(memory_space=pltpu.VMEM)
SMEM = pl.BlockSpec(memory_space=pltpu.SMEM)
PARAMS = pltpu.CompilerParams(vmem_limit_bytes=48 << 20)


def dot1(a, b, dims):
    return lax.dot_general(a.astype(BF16), b.astype(BF16), dims, preferred_element_type=F32)


def split(x):
    hi = x.astype(BF16)
    return hi, (x - hi.astype(F32)).astype(BF16)


def dot3(a, b, dims):
    dot = functools.partial(lax.dot_general, dimension_numbers=dims, preferred_element_type=F32)
    return dot(a[0], b[0]) + (dot(a[0], b[1]) + dot(a[1], b[0]))


def dot_full(a, b, dims):
    return lax.dot_general(a, b, dims, preferred_element_type=F32, precision=lax.Precision.HIGHEST)


def iotas():
    shape = (N, N)
    return lax.broadcasted_iota(jnp.int32, shape, 0), lax.broadcasted_iota(jnp.int32, shape, 1)


def inv_sqrt_diag(m, eye):
    picked = jnp.where(eye, m, 0.0)
    col = lax.rsqrt(jnp.sum(picked, axis=1, keepdims=True))
    row = lax.rsqrt(jnp.sum(picked, axis=0, keepdims=True))
    return col, row


def inverse_factor(m):
    r, c = iotas()
    eye = r == c
    below = r > c
    one = jnp.where(eye, 1.0, 0.0)
    col, start = inv_sqrt_diag(m, eye)
    m = col * m * start
    s = jnp.where(below, m, 0.0)
    s2 = dot1(s, s, NN)
    t = one - s
    x = t + dot1(t, s2, NN)
    for _ in range(2):
        mk = dot1(dot1(x, m, NN), x, NT)
        col, row = inv_sqrt_diag(mk, eye)
        s = jnp.where(below, col * mk * row, 0.0)
        s2 = dot1(s, s, NN)
        t = one - s
        x = col * x
        x = x - dot1(s, x, NN) + dot1(dot1(t, s2, NN), x, NN)
    x = jnp.where(r >= c, x, 0.0)
    xs = split(x)
    mk = dot3(split(dot3(xs, split(m), NN)), xs, NT)
    col, row = inv_sqrt_diag(mk, eye)
    off = jnp.where(eye, 0.0, col * mk * row)
    size = jnp.sum(off * off)
    s = jnp.where(below, off, 0.0)
    x = col * x
    step = s - dot1(s, s, NN)
    x = x - dot3(split(step), split(x), NN)
    return x * start, size


def factor_columns(m_ref, l_ref):
    r, c = iotas()

    def body(j, _):
        m = m_ref[...]
        row = jnp.sum(jnp.where(r == j, m, 0.0), axis=0, keepdims=True)
        col = jnp.sum(jnp.where(c == j, m, 0.0), axis=1, keepdims=True)
        pivot = jnp.sum(jnp.where((r == j) & (c == j), m, 0.0))
        pivot = jnp.full((1, N), pivot, F32)
        row = jnp.where(c[:1] >= j, row, 0.0)
        col = jnp.where(r[:, :1] >= j, col, 0.0)
        m_ref[...] = m - col * (row / pivot)
        l_ref[...] = jnp.where(c == j, col / jnp.sqrt(pivot), l_ref[...])
        return 0

    lax.fori_loop(0, N, body, 0)


def invert_lower(l_ref, x_ref):
    r, c = iotas()
    eye = r == c
    diag = jnp.sum(jnp.where(eye, l_ref[...], 0.0), axis=1, keepdims=True)
    x_ref[...] = jnp.where(eye, 1.0 / diag, 0.0)

    def body(k, _):
        rk, ck = r >> k, c >> k
        off = jnp.where(((rk >> 1) == (ck >> 1)) & (rk > ck), l_ref[...], 0.0)
        x = x_ref[...]
        x_ref[...] = x - dot_full(dot_full(x, off, NN), x, NN)
        return 0

    lax.fori_loop(0, 8, body, 0)


def weights_body(a, b, cross, out_ref, y_ref, z_ref, m_ref, l_ref):
    plain = a is None
    r, c = iotas()
    if plain:
        one = jnp.where(r == c, 1.0, 0.0)
        t0, t1 = one + cross.T, one + cross
        unscale = 1.0
    else:
        top = jnp.max(jnp.where(r == c, jnp.maximum(a, b), 0.0))
        top = jnp.full((1, N), top, F32)
        inv = 1.0 / top
        unscale = lax.rsqrt(top)
        a, b, cross = a * inv, b * inv, cross * inv
        sa, sb = split(a), split(b)
        t0, t1 = a + cross.T, b + cross
    sc = split(cross)

    def times(t0, t1):
        s0, s1 = split(t0), split(t1)
        left, right = dot3(s1, sc, NT), dot3(s0, sc, NN)
        if plain:
            return t0 + left, t1 + right
        return dot3(s0, sa, NN) + left, dot3(s1, sb, NN) + right

    u0, u1 = times(t0, t1)
    v0, v1 = times(u0, u1)
    us0, us1 = split(u0), split(u1)
    m = dot3(split(v0), us0, NT) + dot3(split(v1), us1, NT)
    x, size = inverse_factor(m)
    xs = split(x)
    out_ref[0] = (dot3(xs, us0, NN) * unscale).astype(BF16)
    out_ref[1] = (dot3(xs, us1, NN) * unscale).astype(BF16)
    good = jnp.where(size < 0.01, 1, 0)

    @pl.when(good == 0)
    def _():
        y_ref[0] = t0
        y_ref[1] = t1

        def step(it, _):
            y0, y1 = y_ref[0], y_ref[1]
            left, right = dot_full(y1, cross, NT), dot_full(y0, cross, NN)
            if plain:
                z0, z1 = y0 + left, y1 + right
            else:
                z0, z1 = dot_full(y0, a, NN) + left, dot_full(y1, b, NN) + right
            m_ref[...] = dot_full(z0, y0, NT) + dot_full(z1, y1, NT)
            z_ref[0] = jnp.where(it == 0, z0, y0)
            z_ref[1] = jnp.where(it == 0, z1, y1)
            l_ref[...] = jnp.zeros((N, N), F32)
            factor_columns(m_ref, l_ref)
            invert_lower(l_ref, m_ref)
            xi = m_ref[...]
            y_ref[0] = dot_full(xi, z_ref[0], NN)
            y_ref[1] = dot_full(xi, z_ref[1], NN)
            return 0

        lax.fori_loop(0, 2, step, 0)
        out_ref[0] = (y_ref[0] * unscale).astype(BF16)
        out_ref[1] = (y_ref[1] * unscale).astype(BF16)


SCRATCH = [pltpu.VMEM((2, N, N), F32)] * 2 + [pltpu.VMEM((N, N), F32)] * 2
WEIGHTS = jax.ShapeDtypeStruct((2, N, N), BF16)


def full_kernel(core_ref, mine_ref, theirs_ref, out_ref, g_ref, *scratch):
    core = core_ref[0]
    for y in range(8):
        for k in range(3):
            at = pl.multiple_of(2 * ROWS * y + ROWS * core, ROWS)
            g_ref[k, pl.ds(at, ROWS), :] = mine_ref[y, ROWS * k : ROWS * (k + 1), :]
            at = pl.multiple_of(2 * ROWS * y + ROWS * (1 - core), ROWS)
            g_ref[k, pl.ds(at, ROWS), :] = theirs_ref[y, ROWS * k : ROWS * (k + 1), :]
    weights_body(g_ref[0], g_ref[1], g_ref[2], out_ref, *scratch)


def full_weights(core, mine, theirs):
    return pl.pallas_call(
        full_kernel,
        out_shape=WEIGHTS,
        in_specs=[SMEM, VMEM, VMEM],
        out_specs=VMEM,
        scratch_shapes=[pltpu.VMEM((3, N, N), F32)] + SCRATCH,
        compiler_params=PARAMS,
        name="full_weights",
    )(core, mine, theirs)


def plain_kernel(cross_ref, out_ref, *scratch):
    weights_body(None, None, cross_ref[...].astype(F32), out_ref, *scratch)


def plain_weights(cross):
    return pl.pallas_call(
        plain_kernel,
        out_shape=WEIGHTS,
        in_specs=[VMEM],
        out_specs=VMEM,
        scratch_shapes=SCRATCH,
        compiler_params=PARAMS,
        name="plain_weights",
    )(cross)


def mix_kernel(p_ref, q_ref, w_ref, out_ref):
    out = dot1(p_ref[...], w_ref[0], NT) + dot1(q_ref[...], w_ref[1], NT)
    out_ref[...] = out.astype(BF16)


def mix(p, q, w):
    return pl.pallas_call(
        mix_kernel,
        out_shape=jax.ShapeDtypeStruct(p.shape, BF16),
        in_specs=[VMEM] * 3,
        out_specs=VMEM,
        compiler_params=PARAMS,
        name="mix",
    )(p, q, w)


def mix_cross_kernel(p_ref, q_ref, w_ref, left_ref, out_ref, cross_ref):
    out = dot1(p_ref[...], w_ref[0], NT) + dot1(q_ref[...], w_ref[1], NT)
    out = out.astype(BF16)
    out_ref[...] = out
    cross_ref[...] = dot1(left_ref[...], out, TN).astype(BF16)


def mix_cross(p, q, w, left):
    return pl.pallas_call(
        mix_cross_kernel,
        out_shape=(jax.ShapeDtypeStruct(p.shape, BF16), jax.ShapeDtypeStruct((N, N), BF16)),
        in_specs=[VMEM] * 4,
        out_specs=(VMEM, VMEM),
        compiler_params=PARAMS,
        name="mix_cross",
    )(p, q, w, left)


def gram(a, b):
    return lax.dot_general(a, b, TN, preferred_element_type=F32)


def partner(value, mask):
    return lax.ppermute(value, "grp", [(g, g ^ mask) for g in range(GRP)])


def scatter_sum(value):
    parts = value.reshape((VOX, value.shape[0] // VOX) + value.shape[1:])
    parts = lax.all_to_all(parts, "vox", 0, 0)
    return jnp.sum(parts.astype(F32), axis=0)


def collect(rows):
    sent = jnp.broadcast_to(rows[None], (VOX,) + rows.shape)
    return lax.all_to_all(sent, "vox", 0, 0).reshape((-1,) + rows.shape[1:])


def collect_halves(rows):
    same_core = [[2 * y + c for y in range(8)] for c in range(2)]
    sent = jnp.broadcast_to(rows[None], (8,) + rows.shape)
    mine = lax.all_to_all(sent, "vox", 0, 0, axis_index_groups=same_core)
    return mine, lax.ppermute(mine, "vox", [(v, v ^ 1) for v in range(VOX)])


def tree(own, series):
    core = (lax.axis_index("vox") & 1).astype(jnp.int32).reshape(1)
    other = partner(own, 1)
    own_rows = scatter_sum(gram(own, own))
    own_late, other_late = lax.optimization_barrier((own, other))
    far_own = partner(own_late, 2)
    far_other = partner(other_late, 2)
    other_rows = partner(own_rows, 1)
    cross_rows = scatter_sum(gram(own, other))
    rows = jnp.concatenate([own_rows, other_rows, cross_rows], axis=0)
    mine, theirs = collect_halves(rows)
    w = full_weights(core, mine, theirs)
    far_w = partner(w, 2)
    left = mix(own, other, w)
    deep_left = partner(left, 4)
    right, cross = mix_cross(far_own, far_other, far_w, left)
    deep_right = partner(right, 4)
    rows = scatter_sum(cross)
    cross = collect(rows.astype(BF16))
    w = plain_weights(cross)
    deep_w = partner(w, 4)
    left = mix(left, right, w)
    right, cross = mix_cross(deep_left, deep_right, deep_w, left)
    rows = scatter_sum(cross)
    cross = collect(rows.astype(BF16))
    root = mix(left, right, plain_weights(cross))
    return scatter_sum(gram(root, series).astype(BF16))


def local(group_basis, timeseries):
    return tree(group_basis[0], timeseries[0])[None]


def solution(mesh):
    return jax.shard_map(
        local,
        mesh=mesh,
        in_specs=(P("grp", "vox", None), P("grp", "vox", None)),
        out_specs=P("grp", "vox", None),
        check_vma=False,
    )
```

profile of v0, /device:TPU:1, one launch (start us, length us, event | category | flops | bytes accessed | tf_op | source)
XLA Modules:
  0.0 329.4 jit_solution(15434787492316533014)
XLA Ops:
  0.0 0.0 copy-start
  0.0 4.1 %collective-permute-start = (bf16[1024,256]{1,0:T(8,128)(2,1)}, bf16[1024,256]{1,0:T(8,128)(2,1)S(1)}, u32[]{:S(2)}, u32[]{:S(2)}) collective-permute-start(bf16[1024,256]{1,0:T(8,128)(2,1)} %bitcast.23), channel_id=1, source_target_pairs={{0,16},{16,0},{32,48},{48,32},{64,80},{80,64},{96,112},{112,96},{1... | collective-permute-start | bytes 1572872 | tf_op jit(solution)/shard_map/ppermute | solution.py:266
  4.1 0.0 copy-start.1
  4.1 1.3 copy.5
  5.4 0.0 copy-done.1
  5.4 1.0 fusion.3
  6.4 8.1 %all-to-all-start = ((f32[16,16,256]{2,1,0:T(8,128)}), f32[16,16,256]{2,1,0:T(8,128)S(1)}, u32[]{:S(2)}, u32[]{:S(2)}) async-start(f32[16,16,256]{2,1,0:T(8,128)} %fusion.3), calls=%async_computation | async-start | bytes 524288 | tf_op jit(solution)/shard_map/all_to_all | solution.py:271
  14.6 0.0 collective-permute-done.q_ref
  14.6 1.0 fusion.1
  15.6 10.7 %all-to-all-done = f32[16,16,256]{2,1,0:T(8,128)S(1)} async-done(((f32[16,16,256]{2,1,0:T(8,128)}), f32[16,16,256]{2,1,0:T(8,128)S(1)}, u32[]{:S(2)}, u32[]{:S(2)}) %all-to-all-start) | async-done | bytes 262176 | tf_op jit(solution)/shard_map/all_to_all | solution.py:271
  26.3 3.4 %all-to-all-start.1 = ((f32[16,16,256]{2,1,0:T(8,128)}), f32[16,16,256]{2,1,0:T(8,128)S(1)}, u32[]{:S(2)}, u32[]{:S(2)}) async-start(f32[16,16,256]{2,1,0:T(8,128)} %fusion.1), calls=%async_computation.1 | async-start | bytes 524288 | tf_op jit(solution)/shard_map/all_to_all | solution.py:271
  29.8 3.6 %collective-permute-start.1 = (f32[16,256]{1,0:T(8,128)S(1)}, f32[16,256]{1,0:T(8,128)S(1)}, u32[]{:S(2)}, u32[]{:S(2)}) collective-permute-start(f32[16,256]{1,0:T(8,128)S(1)} %reduce_sum.51), channel_id=1, source_target_pairs={{0,16},{16,0},{32,48},{48,32},{64,80},{80,64},{96,112},{112,96},{1... | collective-permute-start | bytes 49160 | tf_op jit(solution)/shard_map/ppermute | solution.py:266
  33.4 7.3 %all-to-all-done.1 = f32[16,16,256]{2,1,0:T(8,128)S(1)} async-done(((f32[16,16,256]{2,1,0:T(8,128)}), f32[16,16,256]{2,1,0:T(8,128)S(1)}, u32[]{:S(2)}, u32[]{:S(2)}) %all-to-all-start.1) | async-done | bytes 262176 | tf_op jit(solution)/shard_map/all_to_all | solution.py:271
  40.7 0.0 collective-permute-done.1
  40.8 16.8 %all_to_all.40.mine_ref = f32[8,48,256]{2,1,0:T(8,128)S(1)} all-to-all(f32[8,48,256]{2,1,0:T(8,128)S(1)} %broadcast_in_dim.8), channel_id=1, replica_groups={{0,2,4,6,8,10,12,14},{1,3,5,7,9,11,13,15},{16,18,20,22,24,26,28,30},{17..., dimensions={0} | all-to-all | bytes 786432 | tf_op jit(solution)/shard_map/all_to_all | solution.py:283
  57.5 3.2 collective-permute-start.2
  60.7 4.3 %collective-permute-start.3 = (bf16[1024,256]{1,0:T(8,128)(2,1)S(1)}, bf16[1024,256]{1,0:T(8,128)(2,1)S(1)}, u32[]{:S(2)}, u32[]{:S(2)}) collective-permute-start(bf16[1024,256]{1,0:T(8,128)(2,1)S(1)} %bitcast.25), channel_id=1, source_target_pairs={{0,32},{16,48},{32,0},{48,16},{64,96},{80,112},{96,64},{112,80},{1... | collective-permute-start | bytes 1572872 | tf_op jit(solution)/shard_map/ppermute | solution.py:266
  65.0 2.5 collective-permute-start.4
  67.5 0.0 collective-permute-done.2.theirs_ref
  67.5 160.6 %full_weights.1.w_ref = bf16[2,256,256]{2,1,0:T(8,128)(2,1)S(1)} custom-call(s32[1]{0:T(128)} %bitcast.1.core_ref, f32[8,48,256]{2,1,0:T(8,128)S(1)} %all_to_all.40.mine_ref, f32[8,48,256]{2,1,0:T(8,128)S(1)} %collective-permute-done.2.theirs_ref), custom_call_target="tpu_custom_call" | custom-call | tf_op jit(solution)/shard_map/full_weights/pallas_call | solution.py:200
  228.1 4.3 %collective-permute-start.5 = (bf16[2,256,256]{2,1,0:T(8,128)(2,1)S(1)}, bf16[2,256,256]{2,1,0:T(8,128)(2,1)S(1)}, u32[]{:S(2)}, u32[]{:S(2)}) collective-permute-start(bf16[2,256,256]{2,1,0:T(8,128)(2,1)S(1)} %full_weights.1.w_ref), channel_id=1, source_target_pairs={{0,32},{16,48},{32,0},{48,16},{64,96},{80,112},{96,64},{112,80},{1... | collective-permute-start | bytes 786440 | tf_op jit(solution)/shard_map/ppermute | solution.py:266
  232.5 0.5 mix.3.left_ref.p_ref
  232.9 0.0 collective-permute-done.3.p_ref
  232.9 0.0 collective-permute-done.4.q_ref
  232.9 5.8 %collective-permute-done.5.w_ref = bf16[2,256,256]{2,1,0:T(8,128)(2,1)S(1)} collective-permute-done((bf16[2,256,256]{2,1,0:T(8,128)(2,1)S(1)}, bf16[2,256,256]{2,1,0:T(8,128)(2,1)S(1)}, u32[]{:S(2)}, u32[]{:S(2)}) %collective-permute-start.5) | collective-permute-done | bytes 262176 | tf_op jit(solution)/shard_map/ppermute | solution.py:266
  238.8 2.5 mix_cross.2
  241.3 4.7 %all-to-all-start.3 = ((bf16[16,16,256]{2,1,0:T(8,128)(2,1)}), bf16[16,16,256]{2,1,0:T(8,128)(2,1)S(1)}, u32[]{:S(2)}, u32[]{:S(2)}) async-start(bf16[16,16,256]{2,1,0:T(8,128)(2,1)} %bitcast.6), calls=%async_computation.3 | async-start | bytes 262144 | tf_op jit(solution)/shard_map/all_to_all | solution.py:271
  246.0 4.0 %collective-permute-start.6 = (bf16[1024,256]{1,0:T(8,128)(2,1)S(1)}, bf16[1024,256]{1,0:T(8,128)(2,1)S(1)}, u32[]{:S(2)}, u32[]{:S(2)}) collective-permute-start(bf16[1024,256]{1,0:T(8,128)(2,1)S(1)} %mix.3.left_ref.p_ref), channel_id=1, source_target_pairs={{0,64},{16,80},{32,96},{48,112},{64,0},{80,16},{96,32},{112,48},{1... | collective-permute-start | bytes 1572872 | tf_op jit(solution)/shard_map/ppermute | solution.py:266
  250.0 1.9 collective-permute-start.7
  251.9 3.3 all-to-all-done.3
  255.2 13.0 %all_to_all.41 = bf16[16,16,256]{2,1,0:T(8,128)(2,1)S(1)} all-to-all(bf16[16,16,256]{2,1,0:T(8,128)(2,1)S(1)} %broadcast_in_dim.9), channel_id=1, replica_groups=mesh['grp'=32,'vox'=16] {'vox'}, dimensions={0} | all-to-all | bytes 262144 | tf_op jit(solution)/shard_map/all_to_all | solution.py:277
  268.2 4.6 %plain_weights.2.w_ref = bf16[2,256,256]{2,1,0:T(8,128)(2,1)S(1)} custom-call(bf16[256,256]{1,0:T(8,128)(2,1)S(1)} %bitcast.27), custom_call_target="tpu_custom_call" | custom-call | tf_op jit(solution)/shard_map/plain_weights/pallas_call | solution.py:216
  272.8 3.6 %collective-permute-start.8 = (bf16[2,256,256]{2,1,0:T(8,128)(2,1)S(1)}, bf16[2,256,256]{2,1,0:T(8,128)(2,1)S(1)}, u32[]{:S(2)}, u32[]{:S(2)}) collective-permute-start(bf16[2,256,256]{2,1,0:T(8,128)(2,1)S(1)} %plain_weights.2.w_ref), channel_id=1, source_target_pairs={{0,64},{16,80},{32,96},{48,112},{64,0},{80,16},{96,32},{112,48},{1... | collective-permute-start | bytes 786440 | tf_op jit(solution)/shard_map/ppermute | solution.py:266
  276.5 0.5 mix.4.left_ref.p_ref
  277.0 0.0 collective-permute-done.6.p_ref
  277.0 0.0 collective-permute-done.7.q_ref
  277.0 6.3 %collective-permute-done.8.w_ref = bf16[2,256,256]{2,1,0:T(8,128)(2,1)S(1)} collective-permute-done((bf16[2,256,256]{2,1,0:T(8,128)(2,1)S(1)}, bf16[2,256,256]{2,1,0:T(8,128)(2,1)S(1)}, u32[]{:S(2)}, u32[]{:S(2)}) %collective-permute-start.8) | collective-permute-done | bytes 262176 | tf_op jit(solution)/shard_map/ppermute | solution.py:266
  283.3 1.8 mix_cross.3
  285.1 12.0 %all_to_all.42 = bf16[16,16,256]{2,1,0:T(8,128)(2,1)S(1)} all-to-all(bf16[16,16,256]{2,1,0:T(8,128)(2,1)S(1)} %bitcast.29), channel_id=1, replica_groups=mesh['grp'=32,'vox'=16] {'vox'}, dimensions={0} | all-to-all | bytes 262144 | tf_op jit(solution)/shard_map/all_to_all | solution.py:271
  297.1 11.6 %all_to_all.43 = bf16[16,16,256]{2,1,0:T(8,128)(2,1)S(1)} all-to-all(bf16[16,16,256]{2,1,0:T(8,128)(2,1)S(1)} %broadcast_in_dim.10), channel_id=1, replica_groups=mesh['grp'=32,'vox'=16] {'vox'}, dimensions={0} | all-to-all | bytes 262144 | tf_op jit(solution)/shard_map/all_to_all | solution.py:277
  308.7 4.9 %plain_weights.3.w_ref = bf16[2,256,256]{2,1,0:T(8,128)(2,1)S(1)} custom-call(bf16[256,256]{1,0:T(8,128)(2,1)S(1)} %bitcast.28), custom_call_target="tpu_custom_call" | custom-call | tf_op jit(solution)/shard_map/plain_weights/pallas_call | solution.py:216
  313.5 0.5 mix.5
  314.0 0.0 copy-done
  314.0 0.5 convolution_convert_fusion
  314.5 14.3 %all_to_all.44 = bf16[16,16,512]{2,1,0:T(8,128)(2,1)S(1)} all-to-all(bf16[16,16,512]{2,1,0:T(8,128)(2,1)S(1)} %bitcast.32), channel_id=1, replica_groups=mesh['grp'=32,'vox'=16] {'vox'}, dimensions={0} | all-to-all | bytes 524288 | tf_op jit(solution)/shard_map/all_to_all | solution.py:271
  328.7 0.7 convert_reduce_fusion
  (8 shorter events, 0.2 us)
Async XLA Ops:
  0.0 314.0 %copy-start = (bf16[1,1024,512]{2,1,0:T(8,128)(2,1)S(1)}, bf16[1,1024,512]{2,1,0:T(8,128)(2,1)}, u32[]{:S(2)}) copy-start(bf16[1,1024,512]{2,1,0:T(8,128)(2,1)} %param.3) | copy-start | bytes 3145732
  0.0 14.6 %collective-permute-start = (bf16[1024,256]{1,0:T(8,128)(2,1)}, bf16[1024,256]{1,0:T(8,128)(2,1)S(1)}, u32[]{:S(2)}, u32[]{:S(2)}) collective-permute-start(bf16[1024,256]{1,0:T(8,128)(2,1)} %bitcast.23), channel_id=1, source_target_pairs={{0,16},{16,0},{32,48},{48,32},{64,80},{80,64},{96,112},{112,96},{1... | collective-permute-start | bytes 1572872 | tf_op jit(solution)/shard_map/ppermute | solution.py:266
  4.1 1.3 copy-start.1
  6.4 19.9 %all-to-all-start = ((f32[16,16,256]{2,1,0:T(8,128)}), f32[16,16,256]{2,1,0:T(8,128)S(1)}, u32[]{:S(2)}, u32[]{:S(2)}) async-start(f32[16,16,256]{2,1,0:T(8,128)} %fusion.3), calls=%async_computation | async-start | bytes 524288 | tf_op jit(solution)/shard_map/all_to_all | solution.py:271
  26.3 14.4 %all-to-all-start.1 = ((f32[16,16,256]{2,1,0:T(8,128)}), f32[16,16,256]{2,1,0:T(8,128)S(1)}, u32[]{:S(2)}, u32[]{:S(2)}) async-start(f32[16,16,256]{2,1,0:T(8,128)} %fusion.1), calls=%async_computation.1 | async-start | bytes 524288 | tf_op jit(solution)/shard_map/all_to_all | solution.py:271
  29.8 10.9 %collective-permute-start.1 = (f32[16,256]{1,0:T(8,128)S(1)}, f32[16,256]{1,0:T(8,128)S(1)}, u32[]{:S(2)}, u32[]{:S(2)}) collective-permute-start(f32[16,256]{1,0:T(8,128)S(1)} %reduce_sum.51), channel_id=1, source_target_pairs={{0,16},{16,0},{32,48},{48,32},{64,80},{80,64},{96,112},{112,96},{1... | collective-permute-start | bytes 49160 | tf_op jit(solution)/shard_map/ppermute | solution.py:266
  57.5 10.0 %collective-permute-start.2 = (f32[8,48,256]{2,1,0:T(8,128)S(1)}, f32[8,48,256]{2,1,0:T(8,128)S(1)}, u32[]{:S(2)}, u32[]{:S(2)}) collective-permute-start(f32[8,48,256]{2,1,0:T(8,128)S(1)} %all_to_all.40.mine_ref), channel_id=1, source_target_pairs={{0,1},{1,0},{2,3},{3,2},{4,5},{5,4},{6,7},{7,6},{8,9},{9,8},{10,11... | collective-permute-start | bytes 1179656 | tf_op jit(solution)/shard_map/ppermute | solution.py:284
  60.7 172.2 %collective-permute-start.3 = (bf16[1024,256]{1,0:T(8,128)(2,1)S(1)}, bf16[1024,256]{1,0:T(8,128)(2,1)S(1)}, u32[]{:S(2)}, u32[]{:S(2)}) collective-permute-start(bf16[1024,256]{1,0:T(8,128)(2,1)S(1)} %bitcast.25), channel_id=1, source_target_pairs={{0,32},{16,48},{32,0},{48,16},{64,96},{80,112},{96,64},{112,80},{1... | collective-permute-start | bytes 1572872 | tf_op jit(solution)/shard_map/ppermute | solution.py:266
  65.0 167.9 %collective-permute-start.4 = (bf16[1024,256]{1,0:T(8,128)(2,1)S(1)}, bf16[1024,256]{1,0:T(8,128)(2,1)}, u32[]{:S(2)}, u32[]{:S(2)}) collective-permute-start(bf16[1024,256]{1,0:T(8,128)(2,1)S(1)} %collective-permute-done.q_ref), channel_id=1, source_target_pairs={{0,32},{16,48},{32,0},{48,16},{64,96},{80,112},{96,64},{112,80},{1... | collective-permute-start | bytes 1572872 | tf_op jit(solution)/shard_map/ppermute | solution.py:266
  228.1 10.7 %collective-permute-start.5 = (bf16[2,256,256]{2,1,0:T(8,128)(2,1)S(1)}, bf16[2,256,256]{2,1,0:T(8,128)(2,1)S(1)}, u32[]{:S(2)}, u32[]{:S(2)}) collective-permute-start(bf16[2,256,256]{2,1,0:T(8,128)(2,1)S(1)} %full_weights.1.w_ref), channel_id=1, source_target_pairs={{0,32},{16,48},{32,0},{48,16},{64,96},{80,112},{96,64},{112,80},{1... | collective-permute-start | bytes 786440 | tf_op jit(solution)/shard_map/ppermute | solution.py:266
  241.3 13.9 %all-to-all-start.3 = ((bf16[16,16,256]{2,1,0:T(8,128)(2,1)}), bf16[16,16,256]{2,1,0:T(8,128)(2,1)S(1)}, u32[]{:S(2)}, u32[]{:S(2)}) async-start(bf16[16,16,256]{2,1,0:T(8,128)(2,1)} %bitcast.6), calls=%async_computation.3 | async-start | bytes 262144 | tf_op jit(solution)/shard_map/all_to_all | solution.py:271
  246.0 31.0 %collective-permute-start.6 = (bf16[1024,256]{1,0:T(8,128)(2,1)S(1)}, bf16[1024,256]{1,0:T(8,128)(2,1)S(1)}, u32[]{:S(2)}, u32[]{:S(2)}) collective-permute-start(bf16[1024,256]{1,0:T(8,128)(2,1)S(1)} %mix.3.left_ref.p_ref), channel_id=1, source_target_pairs={{0,64},{16,80},{32,96},{48,112},{64,0},{80,16},{96,32},{112,48},{1... | collective-permute-start | bytes 1572872 | tf_op jit(solution)/shard_map/ppermute | solution.py:266
  250.0 27.0 %collective-permute-start.7 = (bf16[1024,256]{1,0:T(8,128)(2,1)S(1)}, bf16[1024,256]{1,0:T(8,128)(2,1)}, u32[]{:S(2)}, u32[]{:S(2)}) collective-permute-start(bf16[1024,256]{1,0:T(8,128)(2,1)S(1)} %get-tuple-element.13.q_ref), channel_id=1, source_target_pairs={{0,64},{16,80},{32,96},{48,112},{64,0},{80,16},{96,32},{112,48},{1... | collective-permute-start | bytes 1572872 | tf_op jit(solution)/shard_map/ppermute | solution.py:266
  272.8 10.5 %collective-permute-start.8 = (bf16[2,256,256]{2,1,0:T(8,128)(2,1)S(1)}, bf16[2,256,256]{2,1,0:T(8,128)(2,1)S(1)}, u32[]{:S(2)}, u32[]{:S(2)}) collective-permute-start(bf16[2,256,256]{2,1,0:T(8,128)(2,1)S(1)} %plain_weights.2.w_ref), channel_id=1, source_target_pairs={{0,64},{16,80},{32,96},{48,112},{64,0},{80,16},{96,32},{112,48},{1... | collective-permute-start | bytes 786440 | tf_op jit(solution)/shard_map/ppermute | solution.py:266
where the time goes:
time: 330 us; the launch traced here: 329 us
  Pallas kernels  176 us (53%)
  blocking collectives  67.5 us (20%)
  starting transfers between devices  47.8 us (14%)
  waiting for transfers between devices  33.5 us (10%)
    pallas_call x1, Pallas kernels, full_weights(): pl.pallas_call(full_kernel, out_shape=WEIGHTS, in_specs=[SMEM, VMEM, VMEM...  161 us
    ppermute x8, starting transfers between devices, partner(): return lax.ppermute(value, 'grp', [(g, g ^ mask) for g in range(GRP)])  28.4 us
    all_to_all x2, blocking collectives, scatter_sum(): parts = lax.all_to_all(parts, 'vox', 0, 0)  26.2 us
    all_to_all x2, blocking collectives, collect(): return lax.all_to_all(sent, 'vox', 0, 0).reshape((-1,) + rows.shape[1:])  24.5 us
    all_to_all x3, waiting for transfers between devices, scatter_sum(): parts = lax.all_to_all(parts, 'vox', 0, 0)  21.3 us
    all_to_all x1, blocking collectives, collect_halves(): mine = lax.all_to_all(sent, 'vox', 0, 0, axis_index_groups=same_core)  16.8 us
    all_to_all x3, starting transfers between devices, scatter_sum(): parts = lax.all_to_all(parts, 'vox', 0, 0)  16.3 us
    ppermute x8, waiting for transfers between devices, partner(): return lax.ppermute(value, 'grp', [(g, g ^ mask) for g in range(GRP)])  12.2 us
  transfers between devices with their start and end apart: 12, of which 5 were waited for; matrix products, arithmetic and copies ran while one was open for 1% of the time, Pallas kernels for 50%

commit v1 on v0

--- a/solution.py
+++ b/solution.py
@@ -9,6 +9,7 @@
 
 
 N = 256
+H = 128
 VOX = 16
 GRP = 32
 ROWS = N // VOX
@@ -20,7 +21,7 @@
 TN = (((0,), (0,)), ((), ()))
 VMEM = pl.BlockSpec(memory_space=pltpu.VMEM)
 SMEM = pl.BlockSpec(memory_space=pltpu.SMEM)
-PARAMS = pltpu.CompilerParams(vmem_limit_bytes=48 << 20)
+PARAMS = pltpu.CompilerParams(vmem_limit_bytes=16 << 20)
 
 
 def dot1(a, b, dims):
@@ -185,15 +186,23 @@
 WEIGHTS = jax.ShapeDtypeStruct((2, N, N), BF16)
 
 
-def full_kernel(core_ref, mine_ref, theirs_ref, out_ref, g_ref, *scratch):
+def full_kernel(core_ref, mine_ref, theirs_ref, out_ref, a_ref, c_ref, *scratch):
     core = core_ref[0]
-    for y in range(8):
-        for k in range(3):
-            at = pl.multiple_of(2 * ROWS * y + ROWS * core, ROWS)
-            g_ref[k, pl.ds(at, ROWS), :] = mine_ref[y, ROWS * k : ROWS * (k + 1), :]
-            at = pl.multiple_of(2 * ROWS * y + ROWS * (1 - core), ROWS)
-            g_ref[k, pl.ds(at, ROWS), :] = theirs_ref[y, ROWS * k : ROWS * (k + 1), :]
-    weights_body(g_ref[0], g_ref[1], g_ref[2], out_ref, *scratch)
+    for half, ref in ((core, mine_ref), (1 - core, theirs_ref)):
+        for y in range(8):
+            block = 2 * y + half
+            lo = pl.ds(pl.multiple_of(8 * block, 8), 8)
+            hi = pl.ds(pl.multiple_of(H + 8 * block, 8), 8)
+            for k in range(2):
+                a_ref[k, lo, :H] = ref[y, 24 * k : 24 * k + 8, :]
+                a_ref[k, hi, H:] = ref[y, 24 * k + 8 : 24 * k + 16, :]
+                a_ref[k, hi, :H] = ref[y, 24 * k + 16 : 24 * k + 24, :]
+            at = pl.ds(pl.multiple_of(ROWS * block, ROWS), ROWS)
+            c_ref[at, :H] = ref[y, 48:64, :]
+            c_ref[at, H:] = ref[y, 64:80, :]
+    for k in range(2):
+        a_ref[k, :H, H:] = a_ref[k, H:, :H].T
+    weights_body(a_ref[0], a_ref[1], c_ref[...], out_ref, *scratch)
 
 
 def full_weights(core, mine, theirs):
@@ -202,7 +211,7 @@
         out_shape=WEIGHTS,
         in_specs=[SMEM, VMEM, VMEM],
         out_specs=VMEM,
-        scratch_shapes=[pltpu.VMEM((3, N, N), F32)] + SCRATCH,
+        scratch_shapes=[pltpu.VMEM((2, N, N), F32), pltpu.VMEM((N, N), F32)] + SCRATCH,
         compiler_params=PARAMS,
         name="full_weights",
     )(core, mine, theirs)
@@ -240,77 +249,142 @@
     )(p, q, w)
 
 
-def mix_cross_kernel(p_ref, q_ref, w_ref, left_ref, out_ref, cross_ref):
+def project_kernel(p_ref, q_ref, w_ref, *refs):
+    sides, (out_ref, proj_ref) = refs[:-2], refs[-2:]
     out = dot1(p_ref[...], w_ref[0], NT) + dot1(q_ref[...], w_ref[1], NT)
     out = out.astype(BF16)
     out_ref[...] = out
-    cross_ref[...] = dot1(left_ref[...], out, TN).astype(BF16)
-
-
-def mix_cross(p, q, w, left):
-    return pl.pallas_call(
-        mix_cross_kernel,
-        out_shape=(jax.ShapeDtypeStruct(p.shape, BF16), jax.ShapeDtypeStruct((N, N), BF16)),
-        in_specs=[VMEM] * 4,
+    at = 0
+    for side in sides:
+        width = side.shape[1]
+        got = dot1(out, side[...], TN).astype(BF16)
+        proj_ref[:, :, at : at + width] = got.reshape(VOX, ROWS, width)
+        at += width
+
+
+def project(p, q, w, *sides):
+    width = sum(side.shape[1] for side in sides)
+    return pl.pallas_call(
+        project_kernel,
+        out_shape=(
+            jax.ShapeDtypeStruct(p.shape, BF16),
+            jax.ShapeDtypeStruct((VOX, ROWS, width), BF16),
+        ),
+        in_specs=[VMEM] * (3 + len(sides)),
         out_specs=(VMEM, VMEM),
         compiler_params=PARAMS,
-        name="mix_cross",
-    )(p, q, w, left)
-
-
-def gram(a, b):
-    return lax.dot_general(a, b, TN, preferred_element_type=F32)
+        name="project",
+    )(p, q, w, *sides)
+
+
+def self_gram_kernel(p_ref, out_ref):
+    left, right = p_ref[:, :H], p_ref[:, H:]
+    for k, (a, b) in enumerate(((left, left), (right, right), (right, left))):
+        out_ref[:, 8 * k : 8 * k + 8, :] = dot1(a, b, TN).reshape(VOX, 8, H)
+
+
+def self_gram(p):
+    return pl.pallas_call(
+        self_gram_kernel,
+        out_shape=jax.ShapeDtypeStruct((VOX, 24, H), F32),
+        in_specs=[VMEM],
+        out_specs=VMEM,
+        compiler_params=PARAMS,
+        name="self_gram",
+    )(p)
+
+
+def cross_gram_kernel(p_ref, q_ref, out_ref):
+    got = dot1(p_ref[...], q_ref[...], TN)
+    out_ref[:, :ROWS, :] = got[:, :H].reshape(VOX, ROWS, H)
+    out_ref[:, ROWS:, :] = got[:, H:].reshape(VOX, ROWS, H)
+
+
+def cross_gram(p, q):
+    return pl.pallas_call(
+        cross_gram_kernel,
+        out_shape=jax.ShapeDtypeStruct((VOX, 2 * ROWS, H), F32),
+        in_specs=[VMEM, VMEM],
+        out_specs=VMEM,
+        compiler_params=PARAMS,
+        name="cross_gram",
+    )(p, q)
+
+
+def rows_kernel(parts_ref, w_ref, out_ref):
+    total = jnp.sum(parts_ref[...].astype(F32), axis=0)
+    hi, lo = split(total)
+    got = jnp.zeros((ROWS, N), F32)
+    for k in range(2):
+        at = slice(N * k, N * (k + 1))
+        got = got + (dot1(hi[:, at], w_ref[k], NT) + dot1(lo[:, at], w_ref[k], NT))
+    out_ref[...] = jnp.broadcast_to(got.astype(BF16)[None], out_ref.shape)
+
+
+def cross_rows_of(parts, w):
+    return pl.pallas_call(
+        rows_kernel,
+        out_shape=jax.ShapeDtypeStruct((VOX, ROWS, N), BF16),
+        in_specs=[VMEM, VMEM],
+        out_specs=VMEM,
+        compiler_params=PARAMS,
+        name="cross_rows",
+    )(parts, w)
 
 
 def partner(value, mask):
     return lax.ppermute(value, "grp", [(g, g ^ mask) for g in range(GRP)])
 
 
-def scatter_sum(value):
-    parts = value.reshape((VOX, value.shape[0] // VOX) + value.shape[1:])
-    parts = lax.all_to_all(parts, "vox", 0, 0)
+def exchange(parts):
+    return lax.all_to_all(parts, "vox", 0, 0)
+
+
+def same_core(rows):
+    groups = [[2 * y + c for y in range(8)] for c in range(2)]
+    sent = jnp.broadcast_to(rows[None], (8,) + rows.shape)
+    return lax.all_to_all(sent, "vox", 0, 0, axis_index_groups=groups)
+
+
+def swap_cores(value):
+    return lax.ppermute(value, "vox", [(v, v ^ 1) for v in range(VOX)])
+
+
+def add_up(parts):
     return jnp.sum(parts.astype(F32), axis=0)
-
-
-def collect(rows):
-    sent = jnp.broadcast_to(rows[None], (VOX,) + rows.shape)
-    return lax.all_to_all(sent, "vox", 0, 0).reshape((-1,) + rows.shape[1:])
-
-
-def collect_halves(rows):
-    same_core = [[2 * y + c for y in range(8)] for c in range(2)]
-    sent = jnp.broadcast_to(rows[None], (8,) + rows.shape)
-    mine = lax.all_to_all(sent, "vox", 0, 0, axis_index_groups=same_core)
-    return mine, lax.ppermute(mine, "vox", [(v, v ^ 1) for v in range(VOX)])
 
 
 def tree(own, series):
     core = (lax.axis_index("vox") & 1).astype(jnp.int32).reshape(1)
     other = partner(own, 1)
-    own_rows = scatter_sum(gram(own, own))
-    own_late, other_late = lax.optimization_barrier((own, other))
-    far_own = partner(own_late, 2)
-    far_other = partner(other_late, 2)
+    own_rows = add_up(exchange(self_gram(own)))
+    far_own = partner(own, 2)
+    far_other = partner(other, 2)
     other_rows = partner(own_rows, 1)
-    cross_rows = scatter_sum(gram(own, other))
+    cross_rows = add_up(exchange(cross_gram(own, other)))
     rows = jnp.concatenate([own_rows, other_rows, cross_rows], axis=0)
-    mine, theirs = collect_halves(rows)
+    mine = same_core(rows)
+    theirs = swap_cores(mine)
     w = full_weights(core, mine, theirs)
+
+    left, parts = project(own, other, w, far_own, far_other)
+    parts = exchange(parts)
     far_w = partner(w, 2)
-    left = mix(own, other, w)
+    deep_right = partner(left, 6)
+    cross = exchange(cross_rows_of(parts, far_w))
     deep_left = partner(left, 4)
-    right, cross = mix_cross(far_own, far_other, far_w, left)
-    deep_right = partner(right, 4)
-    rows = scatter_sum(cross)
-    cross = collect(rows.astype(BF16))
-    w = plain_weights(cross)
+    right = mix(far_own, far_other, far_w)
+    w = plain_weights(cross.reshape(N, N))
+
+    left, parts = project(left, right, w, deep_left, deep_right)
+    parts = exchange(parts)
     deep_w = partner(w, 4)
-    left = mix(left, right, w)
-    right, cross = mix_cross(deep_left, deep_right, deep_w, left)
-    rows = scatter_sum(cross)
-    cross = collect(rows.astype(BF16))
-    root = mix(left, right, plain_weights(cross))
-    return scatter_sum(gram(root, series).astype(BF16))
+    cross = exchange(cross_rows_of(parts, deep_w))
+    right = mix(deep_left, deep_right, deep_w)
+    w = plain_weights(cross.reshape(N, N))
+
+    _, parts = project(left, right, w, series)
+    return add_up(exchange(parts))
 
 
 def local(group_basis, timeseries):

time: 330 us -> 338 us (1.024)
  blocking collectives: 67.5 us -> 14.2 us
  starting transfers between devices: 47.8 us -> 77.3 us
  waiting for transfers between devices: 33.5 us -> 58.7 us
  Pallas kernels: 176 us -> 182 us
    all_to_all x5 -> x1, blocking collectives: 67.5 us -> 14.2 us  [exchange(): return lax.all_to_all(parts, 'vox', 0, 0)]
    all_to_all x3 -> x7, starting transfers between devices: 16.3 us -> 46.8 us  [the longest x6 43.3 us: exchange(): return lax.all_to_all(parts, 'vox', 0, 0)]
    all_to_all x3 -> x7, waiting for transfers between devices: 21.3 us -> 42.3 us  [the longest x6 35.4 us: exchange(): return lax.all_to_all(parts, 'vox', 0, 0)]
    pallas_call x2 -> x7, Pallas kernels: 4.28 us -> 10.6 us  [the longest x3 6.67 us: project(): pl.pallas_call(project_kernel, out_shape=(jax.ShapeDtypeStruct(p.shape, B...]
  transfers between devices with their start and end apart: 12 -> 16, of which waited for: 5 -> 9; matrix products, arithmetic and copies ran while one was open for 1% -> 0% of each run, Pallas kernels for 50% -> 50%
where the time goes in v1:
time: 338 us; the launch traced here: 336 us
  Pallas kernels  182 us (54%)
  starting transfers between devices  77.3 us (23%)
  waiting for transfers between devices  58.7 us (17%)
  blocking collectives  14.2 us (4%)
  local copies, waits for them, and re-layouts  3.64 us (1%)
    pallas_call x1, Pallas kernels, full_weights(): pl.pallas_call(full_kernel, out_shape=WEIGHTS, in_specs=[SMEM, VMEM, VMEM...  161 us
    all_to_all x6, starting transfers between devices, exchange(): return lax.all_to_all(parts, 'vox', 0, 0)  43.3 us
    all_to_all x6, waiting for transfers between devices, exchange(): return lax.all_to_all(parts, 'vox', 0, 0)  35.4 us
    ppermute x8, starting transfers between devices, partner(): return lax.ppermute(value, 'grp', [(g, g ^ mask) for g in range(GRP)])  28.2 us
    ppermute x8, waiting for transfers between devices, partner(): return lax.ppermute(value, 'grp', [(g, g ^ mask) for g in range(GRP)])  15.2 us
    all_to_all x1, blocking collectives, exchange(): return lax.all_to_all(parts, 'vox', 0, 0)  14.2 us
    pallas_call x2, Pallas kernels, plain_weights(): pl.pallas_call(plain_kernel, out_shape=WEIGHTS, in_specs=[VMEM], out_spec...  9.48 us
    all_to_all x1, waiting for transfers between devices, same_core(): return lax.all_to_all(sent, 'vox', 0, 0, axis_index_groups=groups)  6.93 us
  transfers between devices with their start and end apart: 16, of which 9 were waited for; matrix products, arithmetic and copies ran while one was open for 0% of the time, Pallas kernels for 50%

profile of v1, /device:TPU:1, one launch (start us, length us, event | category | flops | bytes accessed | tf_op | source)
XLA Modules:
  0.0 336.5 jit_solution(14092565056280824129)
XLA Ops:
  0.0 3.9 %collective-permute-start = (bf16[1024,256]{1,0:T(8,128)(2,1)}, bf16[1024,256]{1,0:T(8,128)(2,1)S(1)}, u32[]{:S(2)}, u32[]{:S(2)}) collective-permute-start(bf16[1024,256]{1,0:T(8,128)(2,1)} %bitcast.6), channel_id=1, source_target_pairs={{0,16},{16,0},{32,48},{48,32},{64,80},{80,64},{96,112},{112,96},{1... | collective-permute-start | bytes 1572872 | tf_op jit(solution)/shard_map/ppermute | solution.py:336
  3.9 1.0 copy-done
  5.0 1.1 self_gram.1
  6.1 8.1 %all-to-all-start = ((f32[16,24,128]{2,1,0:T(8,128)}), f32[16,24,128]{2,1,0:T(8,128)S(1)}, u32[]{:S(2)}, u32[]{:S(2)}) async-start(f32[16,24,128]{2,1,0:T(8,128)} %self_gram.1), calls=%async_computation | async-start | bytes 393216 | tf_op jit(solution)/shard_map/all_to_all | solution.py:340
  14.2 0.0 collective-permute-done.q_ref
  14.2 1.0 cross_gram.1
  15.3 9.2 %all-to-all-done = f32[16,24,128]{2,1,0:T(8,128)S(1)} async-done(((f32[16,24,128]{2,1,0:T(8,128)}), f32[16,24,128]{2,1,0:T(8,128)S(1)}, u32[]{:S(2)}, u32[]{:S(2)}) %all-to-all-start) | async-done | bytes 196640 | tf_op jit(solution)/shard_map/all_to_all | solution.py:340
  24.5 3.4 %all-to-all-start.1 = ((f32[16,32,128]{2,1,0:T(8,128)}), f32[16,32,128]{2,1,0:T(8,128)S(1)}, u32[]{:S(2)}, u32[]{:S(2)}) async-start(f32[16,32,128]{2,1,0:T(8,128)} %cross_gram.1), calls=%async_computation.1 | async-start | bytes 524288 | tf_op jit(solution)/shard_map/all_to_all | solution.py:340
  27.9 3.6 %collective-permute-start.1 = (f32[24,128]{1,0:T(8,128)S(1)}, f32[24,128]{1,0:T(8,128)S(1)}, u32[]{:S(2)}, u32[]{:S(2)}) collective-permute-start(f32[24,128]{1,0:T(8,128)S(1)} %reduce_sum.27), channel_id=1, source_target_pairs={{0,16},{16,0},{32,48},{48,32},{64,80},{80,64},{96,112},{112,96},{1... | collective-permute-start | bytes 36872 | tf_op jit(solution)/shard_map/ppermute | solution.py:336
  31.6 7.5 %all-to-all-done.1 = f32[16,32,128]{2,1,0:T(8,128)S(1)} async-done(((f32[16,32,128]{2,1,0:T(8,128)}), f32[16,32,128]{2,1,0:T(8,128)S(1)}, u32[]{:S(2)}, u32[]{:S(2)}) %all-to-all-start.1) | async-done | bytes 262176 | tf_op jit(solution)/shard_map/all_to_all | solution.py:340
  39.1 0.0 collective-permute-done.1
  39.1 0.7 broadcast_in_dim.4
  39.9 3.4 %all-to-all-start.2 = ((f32[8,80,128]{2,1,0:T(8,128)}), f32[8,80,128]{2,1,0:T(8,128)S(1)}, u32[]{:S(2)}, u32[]{:S(2)}) async-start(f32[8,80,128]{2,1,0:T(8,128)} %broadcast_in_dim.4), calls=%async_computation.2 | async-start | bytes 655360 | tf_op jit(solution)/shard_map/all_to_all | solution.py:346
  43.3 4.3 %collective-permute-start.3 = (bf16[1024,256]{1,0:T(8,128)(2,1)S(1)}, bf16[1024,256]{1,0:T(8,128)(2,1)S(1)}, u32[]{:S(2)}, u32[]{:S(2)}) collective-permute-start(bf16[1024,256]{1,0:T(8,128)(2,1)S(1)} %bitcast.9), channel_id=1, source_target_pairs={{0,32},{16,48},{32,0},{48,16},{64,96},{80,112},{96,64},{112,80},{1... | collective-permute-start | bytes 1572872 | tf_op jit(solution)/shard_map/ppermute | solution.py:336
  47.7 2.5 collective-permute-start.4
  50.1 6.9 %all-to-all-done.2.mine_ref = f32[8,80,128]{2,1,0:T(8,128)S(1)} async-done(((f32[8,80,128]{2,1,0:T(8,128)}), f32[8,80,128]{2,1,0:T(8,128)S(1)}, u32[]{:S(2)}, u32[]{:S(2)}) %all-to-all-start.2) | async-done | bytes 327712 | tf_op jit(solution)/shard_map/all_to_all | solution.py:346
  57.1 2.3 collective-permute-start.2
  59.4 1.2 collective-permute-done.2.theirs_ref
  60.6 160.6 %full_weights.1.w_ref = bf16[2,256,256]{2,1,0:T(8,128)(2,1)S(1)} custom-call(s32[1]{0:T(128)} %bitcast.1.core_ref, f32[8,80,128]{2,1,0:T(8,128)S(1)} %all-to-all-done.2.mine_ref, f32[8,80,128]{2,1,0:T(8,128)S(1)} %collective-permute-done.2.theirs_ref), custom_call_target="tpu_custom_call" | custom-call | tf_op jit(solution)/shard_map/full_weights/pallas_call | solution.py:209
  221.2 0.0 collective-permute-done.3.refs_0_.p_ref
  221.2 0.0 collective-permute-done.4.refs_1_.q_ref
  221.2 1.9 project.3
  223.1 3.7 %all-to-all-start.3 = ((bf16[16,16,512]{2,1,0:T(8,128)(2,1)}), bf16[16,16,512]{2,1,0:T(8,128)(2,1)S(1)}, u32[]{:S(2)}, u32[]{:S(2)}) async-start(bf16[16,16,512]{2,1,0:T(8,128)(2,1)} %get-tuple-element.11), calls=%async_computation.3 | async-start | bytes 524288 | tf_op jit(solution)/shard_map/all_to_all | solution.py:340
  226.8 4.0 %collective-permute-start.6 = (bf16[1024,256]{1,0:T(8,128)(2,1)}, bf16[1024,256]{1,0:T(8,128)(2,1)S(1)}, u32[]{:S(2)}, u32[]{:S(2)}) collective-permute-start(bf16[1024,256]{1,0:T(8,128)(2,1)} %get-tuple-element.10.p_ref), channel_id=1, source_target_pairs={{0,64},{16,80},{32,96},{48,112},{64,0},{80,16},{96,32},{112,48},{1... | collective-permute-start | bytes 1572872 | tf_op jit(solution)/shard_map/ppermute | solution.py:336
  230.8 4.1 %collective-permute-start.7 = (bf16[1024,256]{1,0:T(8,128)(2,1)}, bf16[1024,256]{1,0:T(8,128)(2,1)S(1)}, u32[]{:S(2)}, u32[]{:S(2)}) collective-permute-start(bf16[1024,256]{1,0:T(8,128)(2,1)} %get-tuple-element.10.p_ref), channel_id=1, source_target_pairs={{0,96},{16,112},{32,64},{48,80},{64,32},{80,48},{96,0},{112,16},{1... | collective-permute-start | bytes 1572872 | tf_op jit(solution)/shard_map/ppermute | solution.py:336
  234.9 2.4 collective-permute-start.5
  237.3 8.7 %collective-permute-done.5.w_ref = bf16[2,256,256]{2,1,0:T(8,128)(2,1)S(1)} collective-permute-done((bf16[2,256,256]{2,1,0:T(8,128)(2,1)S(1)}, bf16[2,256,256]{2,1,0:T(8,128)(2,1)S(1)}, u32[]{:S(2)}, u32[]{:S(2)}) %collective-permute-start.5) | collective-permute-done | bytes 262176 | tf_op jit(solution)/shard_map/ppermute | solution.py:336
  246.0 0.9 cross_rows.2
  247.0 19.1 %all-to-all-start.4 = ((bf16[16,16,256]{2,1,0:T(8,128)(2,1)}), bf16[16,16,256]{2,1,0:T(8,128)(2,1)S(1)}, u32[]{:S(2)}, u32[]{:S(2)}) async-start(bf16[16,16,256]{2,1,0:T(8,128)(2,1)} %cross_rows.2), calls=%async_computation.4 | async-start | bytes 262144 | tf_op jit(solution)/shard_map/all_to_all | solution.py:340
  266.1 0.5 mix.2.q_ref
  266.5 8.4 %all-to-all-done.4 = bf16[16,16,256]{2,1,0:T(8,128)(2,1)S(1)} async-done(((bf16[16,16,256]{2,1,0:T(8,128)(2,1)}), bf16[16,16,256]{2,1,0:T(8,128)(2,1)S(1)}, u32[]{:S(2)}, u32[]{:S(2)}) %all-to-all-start.4) | async-done | bytes 131104 | tf_op jit(solution)/shard_map/all_to_all | solution.py:340
  274.9 4.6 %plain_weights.2.w_ref = bf16[2,256,256]{2,1,0:T(8,128)(2,1)S(1)} custom-call(bf16[256,256]{1,0:T(8,128)(2,1)S(1)} %bitcast.12), custom_call_target="tpu_custom_call" | custom-call | tf_op jit(solution)/shard_map/plain_weights/pallas_call | solution.py:225
  279.6 0.0 collective-permute-done.7.refs_1_.q_ref
  279.6 3.0 project.4
  282.6 0.8 copy-done.3
  283.4 3.4 %all-to-all-start.5 = ((bf16[16,16,512]{2,1,0:T(8,128)(2,1)}), bf16[16,16,512]{2,1,0:T(8,128)(2,1)S(1)}, u32[]{:S(2)}, u32[]{:S(2)}) async-start(bf16[16,16,512]{2,1,0:T(8,128)(2,1)} %get-tuple-element.13), calls=%async_computation.5 | async-start | bytes 524288 | tf_op jit(solution)/shard_map/all_to_all | solution.py:340
  286.8 3.4 %collective-permute-start.8 = (bf16[2,256,256]{2,1,0:T(8,128)(2,1)S(1)}, bf16[2,256,256]{2,1,0:T(8,128)(2,1)S(1)}, u32[]{:S(2)}, u32[]{:S(2)}) collective-permute-start(bf16[2,256,256]{2,1,0:T(8,128)(2,1)S(1)} %plain_weights.2.w_ref), channel_id=1, source_target_pairs={{0,64},{16,80},{32,96},{48,112},{64,0},{80,16},{96,32},{112,48},{1... | collective-permute-start | bytes 786440 | tf_op jit(solution)/shard_map/ppermute | solution.py:336
  290.2 6.4 %collective-permute-done.8.w_ref = bf16[2,256,256]{2,1,0:T(8,128)(2,1)S(1)} collective-permute-done((bf16[2,256,256]{2,1,0:T(8,128)(2,1)S(1)}, bf16[2,256,256]{2,1,0:T(8,128)(2,1)S(1)}, u32[]{:S(2)}, u32[]{:S(2)}) %collective-permute-start.8) | collective-permute-done | bytes 262176 | tf_op jit(solution)/shard_map/ppermute | solution.py:336
  296.6 1.9 all-to-all-done.5.parts_ref
  298.5 0.9 cross_rows.3
  299.4 5.6 %all-to-all-start.6 = ((bf16[16,16,256]{2,1,0:T(8,128)(2,1)}), bf16[16,16,256]{2,1,0:T(8,128)(2,1)S(1)}, u32[]{:S(2)}, u32[]{:S(2)}) async-start(bf16[16,16,256]{2,1,0:T(8,128)(2,1)} %cross_rows.3), calls=%async_computation.6 | async-start | bytes 262144 | tf_op jit(solution)/shard_map/all_to_all | solution.py:340
  305.0 0.5 mix.3.q_ref
  305.4 8.4 %all-to-all-done.6 = bf16[16,16,256]{2,1,0:T(8,128)(2,1)S(1)} async-done(((bf16[16,16,256]{2,1,0:T(8,128)(2,1)}), bf16[16,16,256]{2,1,0:T(8,128)(2,1)S(1)}, u32[]{:S(2)}, u32[]{:S(2)}) %all-to-all-start.6) | async-done | bytes 131104 | tf_op jit(solution)/shard_map/all_to_all | solution.py:340
  313.8 4.8 %plain_weights.3.w_ref = bf16[2,256,256]{2,1,0:T(8,128)(2,1)S(1)} custom-call(bf16[256,256]{1,0:T(8,128)(2,1)S(1)} %bitcast.13), custom_call_target="tpu_custom_call" | custom-call | tf_op jit(solution)/shard_map/plain_weights/pallas_call | solution.py:225
  318.7 1.0 copy-done.4
  319.8 1.8 project.5
  321.6 14.2 %all_to_all.40 = bf16[16,16,512]{2,1,0:T(8,128)(2,1)S(1)} all-to-all(bf16[16,16,512]{2,1,0:T(8,128)(2,1)S(1)} %get-tuple-element.14), channel_id=1, replica_groups=mesh['grp'=32,'vox'=16] {'vox'}, dimensions={0} | all-to-all | bytes 524288 | tf_op jit(solution)/shard_map/all_to_all | solution.py:340
  335.8 0.7 convert_reduce_fusion
  (12 shorter events, 0.1 us)
Async XLA Ops:
  0.0 14.2 %collective-permute-start = (bf16[1024,256]{1,0:T(8,128)(2,1)}, bf16[1024,256]{1,0:T(8,128)(2,1)S(1)}, u32[]{:S(2)}, u32[]{:S(2)}) collective-permute-start(bf16[1024,256]{1,0:T(8,128)(2,1)} %bitcast.6), channel_id=1, source_target_pairs={{0,16},{16,0},{32,48},{48,32},{64,80},{80,64},{96,112},{112,96},{1... | collective-permute-start | bytes 1572872 | tf_op jit(solution)/shard_map/ppermute | solution.py:336
  3.9 1.1 copy-start
  5.0 9.2 %copy-start.1 = (bf16[1,1024,256]{2,1,0:T(8,128)(2,1)S(1)}, bf16[1,1024,256]{2,1,0:T(8,128)(2,1)}, u32[]{:S(2)}) copy-start(bf16[1,1024,256]{2,1,0:T(8,128)(2,1)} %param.2) | copy-start | bytes 1572868
  6.1 18.4 %all-to-all-start = ((f32[16,24,128]{2,1,0:T(8,128)}), f32[16,24,128]{2,1,0:T(8,128)S(1)}, u32[]{:S(2)}, u32[]{:S(2)}) async-start(f32[16,24,128]{2,1,0:T(8,128)} %self_gram.1), calls=%async_computation | async-start | bytes 393216 | tf_op jit(solution)/shard_map/all_to_all | solution.py:340
  24.5 14.6 %all-to-all-start.1 = ((f32[16,32,128]{2,1,0:T(8,128)}), f32[16,32,128]{2,1,0:T(8,128)S(1)}, u32[]{:S(2)}, u32[]{:S(2)}) async-start(f32[16,32,128]{2,1,0:T(8,128)} %cross_gram.1), calls=%async_computation.1 | async-start | bytes 524288 | tf_op jit(solution)/shard_map/all_to_all | solution.py:340
  27.9 11.2 %collective-permute-start.1 = (f32[24,128]{1,0:T(8,128)S(1)}, f32[24,128]{1,0:T(8,128)S(1)}, u32[]{:S(2)}, u32[]{:S(2)}) collective-permute-start(f32[24,128]{1,0:T(8,128)S(1)} %reduce_sum.27), channel_id=1, source_target_pairs={{0,16},{16,0},{32,48},{48,32},{64,80},{80,64},{96,112},{112,96},{1... | collective-permute-start | bytes 36872 | tf_op jit(solution)/shard_map/ppermute | solution.py:336
  39.9 17.2 %all-to-all-start.2 = ((f32[8,80,128]{2,1,0:T(8,128)}), f32[8,80,128]{2,1,0:T(8,128)S(1)}, u32[]{:S(2)}, u32[]{:S(2)}) async-start(f32[8,80,128]{2,1,0:T(8,128)} %broadcast_in_dim.4), calls=%async_computation.2 | async-start | bytes 655360 | tf_op jit(solution)/shard_map/all_to_all | solution.py:346
  43.3 177.9 %collective-permute-start.3 = (bf16[1024,256]{1,0:T(8,128)(2,1)S(1)}, bf16[1024,256]{1,0:T(8,128)(2,1)S(1)}, u32[]{:S(2)}, u32[]{:S(2)}) collective-permute-start(bf16[1024,256]{1,0:T(8,128)(2,1)S(1)} %bitcast.9), channel_id=1, source_target_pairs={{0,32},{16,48},{32,0},{48,16},{64,96},{80,112},{96,64},{112,80},{1... | collective-permute-start | bytes 1572872 | tf_op jit(solution)/shard_map/ppermute | solution.py:336
  47.7 173.6 %collective-permute-start.4 = (bf16[1024,256]{1,0:T(8,128)(2,1)S(1)}, bf16[1024,256]{1,0:T(8,128)(2,1)S(1)}, u32[]{:S(2)}, u32[]{:S(2)}) collective-permute-start(bf16[1024,256]{1,0:T(8,128)(2,1)S(1)} %collective-permute-done.q_ref), channel_id=1, source_target_pairs={{0,32},{16,48},{32,0},{48,16},{64,96},{80,112},{96,64},{112,80},{1... | collective-permute-start | bytes 1572872 | tf_op jit(solution)/shard_map/ppermute | solution.py:336
  57.1 3.6 %collective-permute-start.2 = (f32[8,80,128]{2,1,0:T(8,128)S(1)}, f32[8,80,128]{2,1,0:T(8,128)S(1)}, u32[]{:S(2)}, u32[]{:S(2)}) collective-permute-start(f32[8,80,128]{2,1,0:T(8,128)S(1)} %all-to-all-done.2.mine_ref), channel_id=1, source_target_pairs={{0,1},{1,0},{2,3},{3,2},{4,5},{5,4},{6,7},{7,6},{8,9},{9,8},{10,11... | collective-permute-start | bytes 983048 | tf_op jit(solution)/shard_map/ppermute | solution.py:350
  223.1 22.9 %all-to-all-start.3 = ((bf16[16,16,512]{2,1,0:T(8,128)(2,1)}), bf16[16,16,512]{2,1,0:T(8,128)(2,1)S(1)}, u32[]{:S(2)}, u32[]{:S(2)}) async-start(bf16[16,16,512]{2,1,0:T(8,128)(2,1)} %get-tuple-element.11), calls=%async_computation.3 | async-start | bytes 524288 | tf_op jit(solution)/shard_map/all_to_all | solution.py:340
  226.8 52.7 %collective-permute-start.6 = (bf16[1024,256]{1,0:T(8,128)(2,1)}, bf16[1024,256]{1,0:T(8,128)(2,1)S(1)}, u32[]{:S(2)}, u32[]{:S(2)}) collective-permute-start(bf16[1024,256]{1,0:T(8,128)(2,1)} %get-tuple-element.10.p_ref), channel_id=1, source_target_pairs={{0,64},{16,80},{32,96},{48,112},{64,0},{80,16},{96,32},{112,48},{1... | collective-permute-start | bytes 1572872 | tf_op jit(solution)/shard_map/ppermute | solution.py:336
  230.8 48.8 %collective-permute-start.7 = (bf16[1024,256]{1,0:T(8,128)(2,1)}, bf16[1024,256]{1,0:T(8,128)(2,1)S(1)}, u32[]{:S(2)}, u32[]{:S(2)}) collective-permute-start(bf16[1024,256]{1,0:T(8,128)(2,1)} %get-tuple-element.10.p_ref), channel_id=1, source_target_pairs={{0,96},{16,112},{32,64},{48,80},{64,32},{80,48},{96,0},{112,16},{1... | collective-permute-start | bytes 1572872 | tf_op jit(solution)/shard_map/ppermute | solution.py:336
  234.9 11.2 %collective-permute-start.5 = (bf16[2,256,256]{2,1,0:T(8,128)(2,1)S(1)}, bf16[2,256,256]{2,1,0:T(8,128)(2,1)S(1)}, u32[]{:S(2)}, u32[]{:S(2)}) collective-permute-start(bf16[2,256,256]{2,1,0:T(8,128)(2,1)S(1)} %full_weights.1.w_ref), channel_id=1, source_target_pairs={{0,32},{16,48},{32,0},{48,16},{64,96},{80,112},{96,64},{112,80},{1... | collective-permute-start | bytes 786440 | tf_op jit(solution)/shard_map/ppermute | solution.py:336
  247.0 28.0 %all-to-all-start.4 = ((bf16[16,16,256]{2,1,0:T(8,128)(2,1)}), bf16[16,16,256]{2,1,0:T(8,128)(2,1)S(1)}, u32[]{:S(2)}, u32[]{:S(2)}) async-start(bf16[16,16,256]{2,1,0:T(8,128)(2,1)} %cross_rows.2), calls=%async_computation.4 | async-start | bytes 262144 | tf_op jit(solution)/shard_map/all_to_all | solution.py:340
  282.6 0.8 copy-start.3
  283.4 15.1 %all-to-all-start.5 = ((bf16[16,16,512]{2,1,0:T(8,128)(2,1)}), bf16[16,16,512]{2,1,0:T(8,128)(2,1)S(1)}, u32[]{:S(2)}, u32[]{:S(2)}) async-start(bf16[16,16,512]{2,1,0:T(8,128)(2,1)} %get-tuple-element.13), calls=%async_computation.5 | async-start | bytes 524288 | tf_op jit(solution)/shard_map/all_to_all | solution.py:340
  286.8 9.8 %collective-permute-start.8 = (bf16[2,256,256]{2,1,0:T(8,128)(2,1)S(1)}, bf16[2,256,256]{2,1,0:T(8,128)(2,1)S(1)}, u32[]{:S(2)}, u32[]{:S(2)}) collective-permute-start(bf16[2,256,256]{2,1,0:T(8,128)(2,1)S(1)} %plain_weights.2.w_ref), channel_id=1, source_target_pairs={{0,64},{16,80},{32,96},{48,112},{64,0},{80,16},{96,32},{112,48},{1... | collective-permute-start | bytes 786440 | tf_op jit(solution)/shard_map/ppermute | solution.py:336
  299.4 14.5 %all-to-all-start.6 = ((bf16[16,16,256]{2,1,0:T(8,128)(2,1)}), bf16[16,16,256]{2,1,0:T(8,128)(2,1)S(1)}, u32[]{:S(2)}, u32[]{:S(2)}) async-start(bf16[16,16,256]{2,1,0:T(8,128)(2,1)} %cross_rows.3), calls=%async_computation.6 | async-start | bytes 262144 | tf_op jit(solution)/shard_map/all_to_all | solution.py:340
  305.0 13.7 %copy-start.2 = (bf16[1,1024,512]{2,1,0:T(8,128)(2,1)S(1)}, bf16[1,1024,512]{2,1,0:T(8,128)(2,1)}, u32[]{:S(2)}) copy-start(bf16[1,1024,512]{2,1,0:T(8,128)(2,1)} %param.3) | copy-start | bytes 3145732
  318.7 1.0 copy-start.4

commit v2 on v1

--- a/solution.py
+++ b/solution.py
@@ -21,7 +21,11 @@
 TN = (((0,), (0,)), ((), ()))
 VMEM = pl.BlockSpec(memory_space=pltpu.VMEM)
 SMEM = pl.BlockSpec(memory_space=pltpu.SMEM)
-PARAMS = pltpu.CompilerParams(vmem_limit_bytes=16 << 20)
+HBM = pl.BlockSpec(memory_space=pltpu.MemorySpace.HBM)
+
+
+def params(mib):
+    return pltpu.CompilerParams(vmem_limit_bytes=mib << 20)
 
 
 def dot1(a, b, dims):
@@ -212,7 +216,7 @@
         in_specs=[SMEM, VMEM, VMEM],
         out_specs=VMEM,
         scratch_shapes=[pltpu.VMEM((2, N, N), F32), pltpu.VMEM((N, N), F32)] + SCRATCH,
-        compiler_params=PARAMS,
+        compiler_params=params(12),
         name="full_weights",
     )(core, mine, theirs)
 
@@ -228,7 +232,7 @@
         in_specs=[VMEM],
         out_specs=VMEM,
         scratch_shapes=SCRATCH,
-        compiler_params=PARAMS,
+        compiler_params=params(12),
         name="plain_weights",
     )(cross)
 
@@ -244,37 +248,62 @@
         out_shape=jax.ShapeDtypeStruct(p.shape, BF16),
         in_specs=[VMEM] * 3,
         out_specs=VMEM,
-        compiler_params=PARAMS,
+        compiler_params=params(6),
         name="mix",
     )(p, q, w)
 
 
-def project_kernel(p_ref, q_ref, w_ref, *refs):
-    sides, (out_ref, proj_ref) = refs[:-2], refs[-2:]
+def project_kernel(p_ref, q_ref, w_ref, r_ref, s_ref, out_hbm, proj_ref, out_ref, sem):
     out = dot1(p_ref[...], w_ref[0], NT) + dot1(q_ref[...], w_ref[1], NT)
     out = out.astype(BF16)
     out_ref[...] = out
-    at = 0
-    for side in sides:
-        width = side.shape[1]
+    copy = pltpu.make_async_copy(out_ref, out_hbm, sem)
+    copy.start()
+    for k, side in enumerate((r_ref, s_ref)):
         got = dot1(out, side[...], TN).astype(BF16)
-        proj_ref[:, :, at : at + width] = got.reshape(VOX, ROWS, width)
-        at += width
-
-
-def project(p, q, w, *sides):
-    width = sum(side.shape[1] for side in sides)
+        proj_ref[:, :, N * k : N * (k + 1)] = got.reshape(VOX, ROWS, N)
+    copy.wait()
+
+
+def project(p, q, w, r, s):
     return pl.pallas_call(
         project_kernel,
         out_shape=(
             jax.ShapeDtypeStruct(p.shape, BF16),
-            jax.ShapeDtypeStruct((VOX, ROWS, width), BF16),
+            jax.ShapeDtypeStruct((VOX, ROWS, 2 * N), BF16),
         ),
-        in_specs=[VMEM] * (3 + len(sides)),
-        out_specs=(VMEM, VMEM),
-        compiler_params=PARAMS,
+        in_specs=[VMEM] * 5,
+        out_specs=(HBM, VMEM),
+        scratch_shapes=[pltpu.VMEM(p.shape, BF16), pltpu.SemaphoreType.DMA],
+        compiler_params=params(8),
         name="project",
-    )(p, q, w, *sides)
+    )(p, q, w, r, s)
+
+
+def load_kernel(p_hbm, q_ref, w_ref, series_hbm, out_ref, p_ref, series_ref, p_sem, sem):
+    first = pltpu.make_async_copy(p_hbm, p_ref, p_sem)
+    first.start()
+    copy = pltpu.make_async_copy(series_hbm, series_ref, sem)
+    copy.start()
+    root = dot1(q_ref[...], w_ref[1], NT)
+    first.wait()
+    root = (root + dot1(p_ref[...], w_ref[0], NT)).astype(BF16)
+    copy.wait()
+    got = dot1(root, series_ref[...], TN).astype(BF16)
+    out_ref[...] = got.reshape(out_ref.shape)
+
+
+def load(p, q, w, series):
+    return pl.pallas_call(
+        load_kernel,
+        out_shape=jax.ShapeDtypeStruct((VOX, ROWS, series.shape[1]), BF16),
+        in_specs=[HBM, VMEM, VMEM, HBM],
+        out_specs=VMEM,
+        scratch_shapes=[pltpu.VMEM(p.shape, BF16), pltpu.VMEM(series.shape, BF16)]
+        + [pltpu.SemaphoreType.DMA] * 2,
+        compiler_params=params(8),
+        name="load",
+    )(p, q, w, series)
 
 
 def self_gram_kernel(p_ref, out_ref):
@@ -289,7 +318,7 @@
         out_shape=jax.ShapeDtypeStruct((VOX, 24, H), F32),
         in_specs=[VMEM],
         out_specs=VMEM,
-        compiler_params=PARAMS,
+        compiler_params=params(4),
         name="self_gram",
     )(p)
 
@@ -306,7 +335,7 @@
         out_shape=jax.ShapeDtypeStruct((VOX, 2 * ROWS, H), F32),
         in_specs=[VMEM, VMEM],
         out_specs=VMEM,
-        compiler_params=PARAMS,
+        compiler_params=params(6),
         name="cross_gram",
     )(p, q)
 
@@ -327,7 +356,7 @@
         out_shape=jax.ShapeDtypeStruct((VOX, ROWS, N), BF16),
         in_specs=[VMEM, VMEM],
         out_specs=VMEM,
-        compiler_params=PARAMS,
+        compiler_params=params(4),
         name="cross_rows",
     )(parts, w)
 
@@ -358,8 +387,8 @@
     core = (lax.axis_index("vox") & 1).astype(jnp.int32).reshape(1)
     other = partner(own, 1)
     own_rows = add_up(exchange(self_gram(own)))
-    far_own = partner(own, 2)
-    far_other = partner(other, 2)
+    far_own = partner(own, 3)
+    far_other = partner(other, 3)
     other_rows = partner(own_rows, 1)
     cross_rows = add_up(exchange(cross_gram(own, other)))
     rows = jnp.concatenate([own_rows, other_rows, cross_rows], axis=0)
@@ -369,11 +398,11 @@
 
     left, parts = project(own, other, w, far_own, far_other)
     parts = exchange(parts)
-    far_w = partner(w, 2)
-    deep_right = partner(left, 6)
+    far_w = partner(w, 3)
+    deep_left = partner(left, 4)
     cross = exchange(cross_rows_of(parts, far_w))
-    deep_left = partner(left, 4)
     right = mix(far_own, far_other, far_w)
+    deep_right = partner(right, 4)
     w = plain_weights(cross.reshape(N, N))
 
     left, parts = project(left, right, w, deep_left, deep_right)
@@ -383,7 +412,7 @@
     right = mix(deep_left, deep_right, deep_w)
     w = plain_weights(cross.reshape(N, N))
 
-    _, parts = project(left, right, w, series)
+    parts = load(left, right, w, series)
     return add_up(exchange(parts))
 
 

time: 338 us -> 320 us (0.947)
  starting transfers between devices: 77.3 us -> 60.9 us
  blocking collectives: 14.2 us -> 25.8 us
  waiting for transfers between devices: 58.7 us -> 47.2 us
    all_to_all x6 -> x5, starting transfers between devices: 43.3 us -> 28.1 us  [exchange(): return lax.all_to_all(parts, 'vox', 0, 0)]
    all_to_all x1 -> x2, blocking collectives: 14.2 us -> 25.8 us  [exchange(): return lax.all_to_all(parts, 'vox', 0, 0)]
    ppermute x8, waiting for transfers between devices: 15.2 us -> 6.29 us  [partner(): return lax.ppermute(value, 'grp', [(g, g ^ mask) for g in range(GRP)])]
    all_to_all x6 -> x5, waiting for transfers between devices: 35.4 us -> 32.4 us  [exchange(): return lax.all_to_all(parts, 'vox', 0, 0)]
  transfers between devices with their start and end apart: 16 -> 15, of which waited for: 9 -> 8; matrix products, arithmetic and copies ran while one was open for 0% -> 0% of each run, Pallas kernels for 50% -> 53%
where the time goes in v2:
time: 320 us; the launch traced here: 319 us
  Pallas kernels  180 us (56%)
  starting transfers between devices  60.9 us (19%)
  waiting for transfers between devices  47.2 us (15%)
  blocking collectives  25.8 us (8%)
  local copies, waits for them, and re-layouts  4.32 us (1%)
    pallas_call x1, Pallas kernels, full_weights(): pl.pallas_call(full_kernel, out_shape=WEIGHTS, in_specs=[SMEM, VMEM, VMEM...  161 us
    all_to_all x5, waiting for transfers between devices, exchange(): return lax.all_to_all(parts, 'vox', 0, 0)  32.4 us
    all_to_all x5, starting transfers between devices, exchange(): return lax.all_to_all(parts, 'vox', 0, 0)  28.1 us
    ppermute x8, starting transfers between devices, partner(): return lax.ppermute(value, 'grp', [(g, g ^ mask) for g in range(GRP)])  27 us
    all_to_all x2, blocking collectives, exchange(): return lax.all_to_all(parts, 'vox', 0, 0)  25.8 us
    pallas_call x2, Pallas kernels, plain_weights(): pl.pallas_call(plain_kernel, out_shape=WEIGHTS, in_specs=[VMEM], out_spec...  9.48 us
    all_to_all x1, waiting for transfers between devices, same_core(): return lax.all_to_all(sent, 'vox', 0, 0, axis_index_groups=groups)  7.22 us
  transfers between devices with their start and end apart: 15, of which 8 were waited for; matrix products, arithmetic and copies ran while one was open for 0% of the time, Pallas kernels for 53%

profile of v2, /device:TPU:1, one launch (start us, length us, event | category | flops | bytes accessed | tf_op | source)
XLA Modules:
  0.0 318.7 jit_solution(17728193196264476739)
XLA Ops:
  0.0 3.9 %collective-permute-start = (bf16[1024,256]{1,0:T(8,128)(2,1)}, bf16[1024,256]{1,0:T(8,128)(2,1)S(1)}, u32[]{:S(2)}, u32[]{:S(2)}) collective-permute-start(bf16[1024,256]{1,0:T(8,128)(2,1)} %bitcast.6), channel_id=1, source_target_pairs={{0,16},{16,0},{32,48},{48,32},{64,80},{80,64},{96,112},{112,96},{1... | collective-permute-start | bytes 1572872 | tf_op jit(solution)/shard_map/ppermute | solution.py:365
  3.9 1.0 copy-done
  5.0 1.1 self_gram.1
  6.1 8.1 %all-to-all-start = ((f32[16,24,128]{2,1,0:T(8,128)}), f32[16,24,128]{2,1,0:T(8,128)S(1)}, u32[]{:S(2)}, u32[]{:S(2)}) async-start(f32[16,24,128]{2,1,0:T(8,128)} %self_gram.1), calls=%async_computation | async-start | bytes 393216 | tf_op jit(solution)/shard_map/all_to_all | solution.py:369
  14.2 0.0 collective-permute-done.q_ref
  14.2 1.1 cross_gram.1
  15.3 9.2 %all-to-all-done = f32[16,24,128]{2,1,0:T(8,128)S(1)} async-done(((f32[16,24,128]{2,1,0:T(8,128)}), f32[16,24,128]{2,1,0:T(8,128)S(1)}, u32[]{:S(2)}, u32[]{:S(2)}) %all-to-all-start) | async-done | bytes 196640 | tf_op jit(solution)/shard_map/all_to_all | solution.py:369
  24.5 3.4 %all-to-all-start.1 = ((f32[16,32,128]{2,1,0:T(8,128)}), f32[16,32,128]{2,1,0:T(8,128)S(1)}, u32[]{:S(2)}, u32[]{:S(2)}) async-start(f32[16,32,128]{2,1,0:T(8,128)} %cross_gram.1), calls=%async_computation.1 | async-start | bytes 524288 | tf_op jit(solution)/shard_map/all_to_all | solution.py:369
  27.9 3.6 %collective-permute-start.1 = (f32[24,128]{1,0:T(8,128)S(1)}, f32[24,128]{1,0:T(8,128)S(1)}, u32[]{:S(2)}, u32[]{:S(2)}) collective-permute-start(f32[24,128]{1,0:T(8,128)S(1)} %reduce_sum.27), channel_id=1, source_target_pairs={{0,16},{16,0},{32,48},{48,32},{64,80},{80,64},{96,112},{112,96},{1... | collective-permute-start | bytes 36872 | tf_op jit(solution)/shard_map/ppermute | solution.py:365
  31.6 7.5 %all-to-all-done.1 = f32[16,32,128]{2,1,0:T(8,128)S(1)} async-done(((f32[16,32,128]{2,1,0:T(8,128)}), f32[16,32,128]{2,1,0:T(8,128)S(1)}, u32[]{:S(2)}, u32[]{:S(2)}) %all-to-all-start.1) | async-done | bytes 262176 | tf_op jit(solution)/shard_map/all_to_all | solution.py:369
  39.1 0.0 collective-permute-done.1
  39.1 0.8 broadcast_in_dim.4
  39.9 3.4 %all-to-all-start.2 = ((f32[8,80,128]{2,1,0:T(8,128)}), f32[8,80,128]{2,1,0:T(8,128)S(1)}, u32[]{:S(2)}, u32[]{:S(2)}) async-start(f32[8,80,128]{2,1,0:T(8,128)} %broadcast_in_dim.4), calls=%async_computation.2 | async-start | bytes 655360 | tf_op jit(solution)/shard_map/all_to_all | solution.py:375
  43.3 3.7 %collective-permute-start.3 = (bf16[1024,256]{1,0:T(8,128)(2,1)S(1)}, bf16[1024,256]{1,0:T(8,128)(2,1)S(1)}, u32[]{:S(2)}, u32[]{:S(2)}) collective-permute-start(bf16[1024,256]{1,0:T(8,128)(2,1)S(1)} %bitcast.9), channel_id=1, source_target_pairs={{0,48},{16,32},{32,16},{48,0},{64,112},{80,96},{96,80},{112,64},{1... | collective-permute-start | bytes 1572872 | tf_op jit(solution)/shard_map/ppermute | solution.py:365
  47.0 2.8 collective-permute-start.4
  49.9 7.2 %all-to-all-done.2.mine_ref = f32[8,80,128]{2,1,0:T(8,128)S(1)} async-done(((f32[8,80,128]{2,1,0:T(8,128)}), f32[8,80,128]{2,1,0:T(8,128)S(1)}, u32[]{:S(2)}, u32[]{:S(2)}) %all-to-all-start.2) | async-done | bytes 327712 | tf_op jit(solution)/shard_map/all_to_all | solution.py:375
  57.1 2.3 collective-permute-start.2
  59.4 1.2 collective-permute-done.2.theirs_ref
  60.6 160.6 %full_weights.1.w_ref = bf16[2,256,256]{2,1,0:T(8,128)(2,1)S(1)} custom-call(s32[1]{0:T(128)} %bitcast.1.core_ref, f32[8,80,128]{2,1,0:T(8,128)S(1)} %all-to-all-done.2.mine_ref, f32[8,80,128]{2,1,0:T(8,128)S(1)} %collective-permute-done.2.theirs_ref), custom_call_target="tpu_custom_call" | custom-call | tf_op jit(solution)/shard_map/full_weights/pallas_call | solution.py:213
  221.2 3.7 %collective-permute-start.5 = (bf16[2,256,256]{2,1,0:T(8,128)(2,1)S(1)}, bf16[2,256,256]{2,1,0:T(8,128)(2,1)S(1)}, u32[]{:S(2)}, u32[]{:S(2)}) collective-permute-start(bf16[2,256,256]{2,1,0:T(8,128)(2,1)S(1)} %full_weights.1.w_ref), channel_id=1, source_target_pairs={{0,48},{16,32},{32,16},{48,0},{64,112},{80,96},{96,80},{112,64},{1... | collective-permute-start | bytes 786440 | tf_op jit(solution)/shard_map/ppermute | solution.py:365
  224.9 0.0 collective-permute-done.3.r_ref.p_ref
  224.9 0.0 collective-permute-done.4.s_ref.q_ref
  224.9 1.5 project.2
  226.4 0.7 copy-done.5
  227.1 4.0 %all-to-all-start.3 = ((bf16[16,16,512]{2,1,0:T(8,128)(2,1)}), bf16[16,16,512]{2,1,0:T(8,128)(2,1)S(1)}, u32[]{:S(2)}, u32[]{:S(2)}) async-start(bf16[16,16,512]{2,1,0:T(8,128)(2,1)} %copy-done.5), calls=%async_computation.3 | async-start | bytes 524288 | tf_op jit(solution)/shard_map/all_to_all | solution.py:369
  231.1 4.0 %collective-permute-start.6 = (bf16[1024,256]{1,0:T(8,128)(2,1)S(1)}, bf16[1024,256]{1,0:T(8,128)(2,1)S(1)}, u32[]{:S(2)}, u32[]{:S(2)}) collective-permute-start(bf16[1024,256]{1,0:T(8,128)(2,1)S(1)} %get-tuple-element.9.p_ref), channel_id=1, source_target_pairs={{0,64},{16,80},{32,96},{48,112},{64,0},{80,16},{96,32},{112,48},{1... | collective-permute-start | bytes 1572872 | tf_op jit(solution)/shard_map/ppermute | solution.py:365
  235.1 0.5 mix.2.q_ref
  235.6 1.9 collective-permute-start.7
  237.5 5.3 %all-to-all-done.3.parts_ref = bf16[16,16,512]{2,1,0:T(8,128)(2,1)S(1)} async-done(((bf16[16,16,512]{2,1,0:T(8,128)(2,1)}), bf16[16,16,512]{2,1,0:T(8,128)(2,1)S(1)}, u32[]{:S(2)}, u32[]{:S(2)}) %all-to-all-start.3) | async-done | bytes 262176 | tf_op jit(solution)/shard_map/all_to_all | solution.py:369
  242.9 0.3 cross_rows.2
  243.1 11.5 %all_to_all.40 = bf16[16,16,256]{2,1,0:T(8,128)(2,1)S(1)} all-to-all(bf16[16,16,256]{2,1,0:T(8,128)(2,1)S(1)} %cross_rows.2), channel_id=1, replica_groups=mesh['grp'=32,'vox'=16] {'vox'}, dimensions={0} | all-to-all | bytes 262144 | tf_op jit(solution)/shard_map/all_to_all | solution.py:369
  254.7 4.6 %plain_weights.2.w_ref = bf16[2,256,256]{2,1,0:T(8,128)(2,1)S(1)} custom-call(bf16[256,256]{1,0:T(8,128)(2,1)S(1)} %bitcast.13), custom_call_target="tpu_custom_call" | custom-call | tf_op jit(solution)/shard_map/plain_weights/pallas_call | solution.py:229
  259.3 0.0 collective-permute-done.6.r_ref.p_ref
  259.3 2.2 project.3
  261.5 0.8 copy-done.3
  262.3 6.8 %all-to-all-start.5 = ((bf16[16,16,512]{2,1,0:T(8,128)(2,1)}), bf16[16,16,512]{2,1,0:T(8,128)(2,1)S(1)}, u32[]{:S(2)}, u32[]{:S(2)}) async-start(bf16[16,16,512]{2,1,0:T(8,128)(2,1)} %get-tuple-element.12), calls=%async_computation.5 | async-start | bytes 524288 | tf_op jit(solution)/shard_map/all_to_all | solution.py:369
  269.1 3.3 %collective-permute-start.8 = (bf16[2,256,256]{2,1,0:T(8,128)(2,1)S(1)}, bf16[2,256,256]{2,1,0:T(8,128)(2,1)S(1)}, u32[]{:S(2)}, u32[]{:S(2)}) collective-permute-start(bf16[2,256,256]{2,1,0:T(8,128)(2,1)S(1)} %plain_weights.2.w_ref), channel_id=1, source_target_pairs={{0,64},{16,80},{32,96},{48,112},{64,0},{80,16},{96,32},{112,48},{1... | collective-permute-start | bytes 786440 | tf_op jit(solution)/shard_map/ppermute | solution.py:365
  272.4 6.3 %collective-permute-done.8.w_ref = bf16[2,256,256]{2,1,0:T(8,128)(2,1)S(1)} collective-permute-done((bf16[2,256,256]{2,1,0:T(8,128)(2,1)S(1)}, bf16[2,256,256]{2,1,0:T(8,128)(2,1)S(1)}, u32[]{:S(2)}, u32[]{:S(2)}) %collective-permute-start.8) | collective-permute-done | bytes 262176 | tf_op jit(solution)/shard_map/ppermute | solution.py:365
  278.7 2.0 all-to-all-done.5.parts_ref
  280.7 0.9 cross_rows.3
  281.6 5.9 %all-to-all-start.6 = ((bf16[16,16,256]{2,1,0:T(8,128)(2,1)}), bf16[16,16,256]{2,1,0:T(8,128)(2,1)S(1)}, u32[]{:S(2)}, u32[]{:S(2)}) async-start(bf16[16,16,256]{2,1,0:T(8,128)(2,1)} %cross_rows.3), calls=%async_computation.6 | async-start | bytes 262144 | tf_op jit(solution)/shard_map/all_to_all | solution.py:369
  287.4 0.5 mix.3.q_ref
  287.9 8.4 %all-to-all-done.6 = bf16[16,16,256]{2,1,0:T(8,128)(2,1)S(1)} async-done(((bf16[16,16,256]{2,1,0:T(8,128)(2,1)}), bf16[16,16,256]{2,1,0:T(8,128)(2,1)S(1)}, u32[]{:S(2)}, u32[]{:S(2)}) %all-to-all-start.6) | async-done | bytes 131104 | tf_op jit(solution)/shard_map/all_to_all | solution.py:369
  296.3 4.9 %plain_weights.3.w_ref = bf16[2,256,256]{2,1,0:T(8,128)(2,1)S(1)} custom-call(bf16[256,256]{1,0:T(8,128)(2,1)S(1)} %bitcast.12), custom_call_target="tpu_custom_call" | custom-call | tf_op jit(solution)/shard_map/plain_weights/pallas_call | solution.py:229
  301.2 1.0 copy-done.4
  302.2 1.6 load.1
  303.8 14.3 %all_to_all.41 = bf16[16,16,512]{2,1,0:T(8,128)(2,1)S(1)} all-to-all(bf16[16,16,512]{2,1,0:T(8,128)(2,1)S(1)} %load.1), channel_id=1, replica_groups=mesh['grp'=32,'vox'=16] {'vox'}, dimensions={0} | all-to-all | bytes 524288 | tf_op jit(solution)/shard_map/all_to_all | solution.py:369
  318.1 0.7 convert_reduce_fusion
  (13 shorter events, 0.1 us)
Async XLA Ops:
  0.0 14.2 %collective-permute-start = (bf16[1024,256]{1,0:T(8,128)(2,1)}, bf16[1024,256]{1,0:T(8,128)(2,1)S(1)}, u32[]{:S(2)}, u32[]{:S(2)}) collective-permute-start(bf16[1024,256]{1,0:T(8,128)(2,1)} %bitcast.6), channel_id=1, source_target_pairs={{0,16},{16,0},{32,48},{48,32},{64,80},{80,64},{96,112},{112,96},{1... | collective-permute-start | bytes 1572872 | tf_op jit(solution)/shard_map/ppermute | solution.py:365
  3.9 1.1 copy-start
  5.0 9.2 %copy-start.1 = (bf16[1,1024,256]{2,1,0:T(8,128)(2,1)S(1)}, bf16[1,1024,256]{2,1,0:T(8,128)(2,1)}, u32[]{:S(2)}) copy-start(bf16[1,1024,256]{2,1,0:T(8,128)(2,1)} %param.2) | copy-start | bytes 1572868
  6.1 18.4 %all-to-all-start = ((f32[16,24,128]{2,1,0:T(8,128)}), f32[16,24,128]{2,1,0:T(8,128)S(1)}, u32[]{:S(2)}, u32[]{:S(2)}) async-start(f32[16,24,128]{2,1,0:T(8,128)} %self_gram.1), calls=%async_computation | async-start | bytes 393216 | tf_op jit(solution)/shard_map/all_to_all | solution.py:369
  24.5 14.6 %all-to-all-start.1 = ((f32[16,32,128]{2,1,0:T(8,128)}), f32[16,32,128]{2,1,0:T(8,128)S(1)}, u32[]{:S(2)}, u32[]{:S(2)}) async-start(f32[16,32,128]{2,1,0:T(8,128)} %cross_gram.1), calls=%async_computation.1 | async-start | bytes 524288 | tf_op jit(solution)/shard_map/all_to_all | solution.py:369
  27.9 11.2 %collective-permute-start.1 = (f32[24,128]{1,0:T(8,128)S(1)}, f32[24,128]{1,0:T(8,128)S(1)}, u32[]{:S(2)}, u32[]{:S(2)}) collective-permute-start(f32[24,128]{1,0:T(8,128)S(1)} %reduce_sum.27), channel_id=1, source_target_pairs={{0,16},{16,0},{32,48},{48,32},{64,80},{80,64},{96,112},{112,96},{1... | collective-permute-start | bytes 36872 | tf_op jit(solution)/shard_map/ppermute | solution.py:365
  39.9 17.2 %all-to-all-start.2 = ((f32[8,80,128]{2,1,0:T(8,128)}), f32[8,80,128]{2,1,0:T(8,128)S(1)}, u32[]{:S(2)}, u32[]{:S(2)}) async-start(f32[8,80,128]{2,1,0:T(8,128)} %broadcast_in_dim.4), calls=%async_computation.2 | async-start | bytes 655360 | tf_op jit(solution)/shard_map/all_to_all | solution.py:375
  43.3 181.6 %collective-permute-start.3 = (bf16[1024,256]{1,0:T(8,128)(2,1)S(1)}, bf16[1024,256]{1,0:T(8,128)(2,1)S(1)}, u32[]{:S(2)}, u32[]{:S(2)}) collective-permute-start(bf16[1024,256]{1,0:T(8,128)(2,1)S(1)} %bitcast.9), channel_id=1, source_target_pairs={{0,48},{16,32},{32,16},{48,0},{64,112},{80,96},{96,80},{112,64},{1... | collective-permute-start | bytes 1572872 | tf_op jit(solution)/shard_map/ppermute | solution.py:365
  47.0 177.9 %collective-permute-start.4 = (bf16[1024,256]{1,0:T(8,128)(2,1)S(1)}, bf16[1024,256]{1,0:T(8,128)(2,1)S(1)}, u32[]{:S(2)}, u32[]{:S(2)}) collective-permute-start(bf16[1024,256]{1,0:T(8,128)(2,1)S(1)} %collective-permute-done.q_ref), channel_id=1, source_target_pairs={{0,48},{16,32},{32,16},{48,0},{64,112},{80,96},{96,80},{112,64},{1... | collective-permute-start | bytes 1572872 | tf_op jit(solution)/shard_map/ppermute | solution.py:365
  57.1 3.6 %collective-permute-start.2 = (f32[8,80,128]{2,1,0:T(8,128)S(1)}, f32[8,80,128]{2,1,0:T(8,128)S(1)}, u32[]{:S(2)}, u32[]{:S(2)}) collective-permute-start(f32[8,80,128]{2,1,0:T(8,128)S(1)} %all-to-all-done.2.mine_ref), channel_id=1, source_target_pairs={{0,1},{1,0},{2,3},{3,2},{4,5},{5,4},{6,7},{7,6},{8,9},{9,8},{10,11... | collective-permute-start | bytes 983048 | tf_op jit(solution)/shard_map/ppermute | solution.py:379
  221.2 13.9 %collective-permute-start.5 = (bf16[2,256,256]{2,1,0:T(8,128)(2,1)S(1)}, bf16[2,256,256]{2,1,0:T(8,128)(2,1)S(1)}, u32[]{:S(2)}, u32[]{:S(2)}) collective-permute-start(bf16[2,256,256]{2,1,0:T(8,128)(2,1)S(1)} %full_weights.1.w_ref), channel_id=1, source_target_pairs={{0,48},{16,32},{32,16},{48,0},{64,112},{80,96},{96,80},{112,64},{1... | collective-permute-start | bytes 786440 | tf_op jit(solution)/shard_map/ppermute | solution.py:365
  226.4 0.7 copy-start.5
  227.1 15.7 %all-to-all-start.3 = ((bf16[16,16,512]{2,1,0:T(8,128)(2,1)}), bf16[16,16,512]{2,1,0:T(8,128)(2,1)S(1)}, u32[]{:S(2)}, u32[]{:S(2)}) async-start(bf16[16,16,512]{2,1,0:T(8,128)(2,1)} %copy-done.5), calls=%async_computation.3 | async-start | bytes 524288 | tf_op jit(solution)/shard_map/all_to_all | solution.py:369
  231.1 28.2 %collective-permute-start.6 = (bf16[1024,256]{1,0:T(8,128)(2,1)S(1)}, bf16[1024,256]{1,0:T(8,128)(2,1)S(1)}, u32[]{:S(2)}, u32[]{:S(2)}) collective-permute-start(bf16[1024,256]{1,0:T(8,128)(2,1)S(1)} %get-tuple-element.9.p_ref), channel_id=1, source_target_pairs={{0,64},{16,80},{32,96},{48,112},{64,0},{80,16},{96,32},{112,48},{1... | collective-permute-start | bytes 1572872 | tf_op jit(solution)/shard_map/ppermute | solution.py:365
  235.6 23.7 %collective-permute-start.7 = (bf16[1024,256]{1,0:T(8,128)(2,1)S(1)}, bf16[1024,256]{1,0:T(8,128)(2,1)S(1)}, u32[]{:S(2)}, u32[]{:S(2)}) collective-permute-start(bf16[1024,256]{1,0:T(8,128)(2,1)S(1)} %mix.2.q_ref), channel_id=1, source_target_pairs={{0,64},{16,80},{32,96},{48,112},{64,0},{80,16},{96,32},{112,48},{1... | collective-permute-start | bytes 1572872 | tf_op jit(solution)/shard_map/ppermute | solution.py:365
  261.5 0.8 copy-start.3
  262.3 18.3 %all-to-all-start.5 = ((bf16[16,16,512]{2,1,0:T(8,128)(2,1)}), bf16[16,16,512]{2,1,0:T(8,128)(2,1)S(1)}, u32[]{:S(2)}, u32[]{:S(2)}) async-start(bf16[16,16,512]{2,1,0:T(8,128)(2,1)} %get-tuple-element.12), calls=%async_computation.5 | async-start | bytes 524288 | tf_op jit(solution)/shard_map/all_to_all | solution.py:369
  269.1 9.6 %collective-permute-start.8 = (bf16[2,256,256]{2,1,0:T(8,128)(2,1)S(1)}, bf16[2,256,256]{2,1,0:T(8,128)(2,1)S(1)}, u32[]{:S(2)}, u32[]{:S(2)}) collective-permute-start(bf16[2,256,256]{2,1,0:T(8,128)(2,1)S(1)} %plain_weights.2.w_ref), channel_id=1, source_target_pairs={{0,64},{16,80},{32,96},{48,112},{64,0},{80,16},{96,32},{112,48},{1... | collective-permute-start | bytes 786440 | tf_op jit(solution)/shard_map/ppermute | solution.py:365
  281.6 14.7 %all-to-all-start.6 = ((bf16[16,16,256]{2,1,0:T(8,128)(2,1)}), bf16[16,16,256]{2,1,0:T(8,128)(2,1)S(1)}, u32[]{:S(2)}, u32[]{:S(2)}) async-start(bf16[16,16,256]{2,1,0:T(8,128)(2,1)} %cross_rows.3), calls=%async_computation.6 | async-start | bytes 262144 | tf_op jit(solution)/shard_map/all_to_all | solution.py:369
  287.4 13.8 %copy-start.2 = (bf16[1,1024,512]{2,1,0:T(8,128)(2,1)S(1)}, bf16[1,1024,512]{2,1,0:T(8,128)(2,1)}, u32[]{:S(2)}) copy-start(bf16[1,1024,512]{2,1,0:T(8,128)(2,1)} %param.3) | copy-start | bytes 3145732
  301.2 1.0 copy-start.4

commit v3 on v2

--- a/solution.py
+++ b/solution.py
@@ -137,15 +137,16 @@
         inv = 1.0 / top
         unscale = lax.rsqrt(top)
         a, b, cross = a * inv, b * inv, cross * inv
-        sa, sb = split(a), split(b)
+        sa, sb, sc = split(a), split(b), split(cross)
         t0, t1 = a + cross.T, b + cross
-    sc = split(cross)
 
     def times(t0, t1):
         s0, s1 = split(t0), split(t1)
+        if plain:
+            left = dot1(s1[0], cross, NT) + dot1(s1[1], cross, NT)
+            right = dot1(s0[0], cross, NN) + dot1(s0[1], cross, NN)
+            return t0 + left, t1 + right
         left, right = dot3(s1, sc, NT), dot3(s0, sc, NN)
-        if plain:
-            return t0 + left, t1 + right
         return dot3(s0, sa, NN) + left, dot3(s1, sb, NN) + right
 
     u0, u1 = times(t0, t1)
@@ -280,15 +281,12 @@
     )(p, q, w, r, s)
 
 
-def load_kernel(p_hbm, q_ref, w_ref, series_hbm, out_ref, p_ref, series_ref, p_sem, sem):
-    first = pltpu.make_async_copy(p_hbm, p_ref, p_sem)
-    first.start()
-    copy = pltpu.make_async_copy(series_hbm, series_ref, sem)
+def load_kernel(p_hbm, q_ref, w_ref, series_ref, out_ref, p_ref, sem):
+    copy = pltpu.make_async_copy(p_hbm, p_ref, sem)
     copy.start()
     root = dot1(q_ref[...], w_ref[1], NT)
-    first.wait()
+    copy.wait()
     root = (root + dot1(p_ref[...], w_ref[0], NT)).astype(BF16)
-    copy.wait()
     got = dot1(root, series_ref[...], TN).astype(BF16)
     out_ref[...] = got.reshape(out_ref.shape)
 
@@ -297,30 +295,43 @@
     return pl.pallas_call(
         load_kernel,
         out_shape=jax.ShapeDtypeStruct((VOX, ROWS, series.shape[1]), BF16),
-        in_specs=[HBM, VMEM, VMEM, HBM],
-        out_specs=VMEM,
-        scratch_shapes=[pltpu.VMEM(p.shape, BF16), pltpu.VMEM(series.shape, BF16)]
-        + [pltpu.SemaphoreType.DMA] * 2,
+        in_specs=[HBM, VMEM, VMEM, VMEM],
+        out_specs=VMEM,
+        scratch_shapes=[pltpu.VMEM(p.shape, BF16), pltpu.SemaphoreType.DMA],
         compiler_params=params(8),
         name="load",
     )(p, q, w, series)
 
 
-def self_gram_kernel(p_ref, out_ref):
-    left, right = p_ref[:, :H], p_ref[:, H:]
-    for k, (a, b) in enumerate(((left, left), (right, right), (right, left))):
-        out_ref[:, 8 * k : 8 * k + 8, :] = dot1(a, b, TN).reshape(VOX, 8, H)
+def self_gram_kernel(p_hbm, out_ref, p_ref, sems):
+    half = p_hbm.shape[0] // 2
+    copies = []
+    for k in range(2):
+        at = pl.ds(half * k, half)
+        copies.append(pltpu.make_async_copy(p_hbm.at[at], p_ref.at[at], sems.at[k]))
+        copies[-1].start()
+    total = None
+    for k in range(2):
+        copies[k].wait()
+        at = pl.ds(half * k, half)
+        left, right = p_ref[at, :H], p_ref[at, H:]
+        pairs = ((left, left), (right, right), (right, left))
+        got = [dot1(a, b, TN) for a, b in pairs]
+        total = got if total is None else [x + y for x, y in zip(total, got)]
+    for k in range(3):
+        out_ref[:, 8 * k : 8 * k + 8, :] = total[k].reshape(VOX, 8, H)
 
 
 def self_gram(p):
     return pl.pallas_call(
         self_gram_kernel,
         out_shape=jax.ShapeDtypeStruct((VOX, 24, H), F32),
-        in_specs=[VMEM],
-        out_specs=VMEM,
+        in_specs=[HBM],
+        out_specs=VMEM,
+        scratch_shapes=[pltpu.VMEM(p.shape, BF16), pltpu.SemaphoreType.DMA((2,))],
         compiler_params=params(4),
         name="self_gram",
-    )(p)
+    )(pltpu.with_memory_space_constraint(p, pltpu.MemorySpace.HBM))
 
 
 def cross_gram_kernel(p_ref, q_ref, out_ref):
@@ -400,9 +411,9 @@
     parts = exchange(parts)
     far_w = partner(w, 3)
     deep_left = partner(left, 4)
+    deep_right = partner(left, 7)
     cross = exchange(cross_rows_of(parts, far_w))
     right = mix(far_own, far_other, far_w)
-    deep_right = partner(right, 4)
     w = plain_weights(cross.reshape(N, N))
 
     left, parts = project(left, right, w, deep_left, deep_right)

time: 320 us -> 336 us (1.050)
  starting transfers between devices: 60.9 us -> 77.2 us
  blocking collectives: 25.8 us -> 14.3 us
  waiting for transfers between devices: 47.2 us -> 58.1 us
    all_to_all x5 -> x6, starting transfers between devices: 28.1 us -> 43.7 us  [exchange(): return lax.all_to_all(parts, 'vox', 0, 0)]
    all_to_all x2 -> x1, blocking collectives: 25.8 us -> 14.3 us  [exchange(): return lax.all_to_all(parts, 'vox', 0, 0)]
    ppermute x8, waiting for transfers between devices: 6.29 us -> 14.2 us  [partner(): return lax.ppermute(value, 'grp', [(g, g ^ mask) for g in range(GRP)])]
    all_to_all x5 -> x6, waiting for transfers between devices: 32.4 us -> 35.4 us  [exchange(): return lax.all_to_all(parts, 'vox', 0, 0)]
  transfers between devices with their start and end apart: 15 -> 16, of which waited for: 8 -> 9; matrix products, arithmetic and copies ran while one was open for 0% -> 0% of each run, Pallas kernels for 53% -> 51%
where the time goes in v3:
time: 336 us; the launch traced here: 335 us
  Pallas kernels  183 us (54%)
  starting transfers between devices  77.2 us (23%)
  waiting for transfers between devices  58.1 us (17%)
  blocking collectives  14.3 us (4%)
    pallas_call x1, Pallas kernels, full_weights(): pl.pallas_call(full_kernel, out_shape=WEIGHTS, in_specs=[SMEM, VMEM, VMEM...  161 us
    all_to_all x6, starting transfers between devices, exchange(): return lax.all_to_all(parts, 'vox', 0, 0)  43.7 us
    all_to_all x6, waiting for transfers between devices, exchange(): return lax.all_to_all(parts, 'vox', 0, 0)  35.4 us
    ppermute x8, starting transfers between devices, partner(): return lax.ppermute(value, 'grp', [(g, g ^ mask) for g in range(GRP)])  27.7 us
    all_to_all x1, blocking collectives, exchange(): return lax.all_to_all(parts, 'vox', 0, 0)  14.3 us
    ppermute x8, waiting for transfers between devices, partner(): return lax.ppermute(value, 'grp', [(g, g ^ mask) for g in range(GRP)])  14.2 us
    pallas_call x2, Pallas kernels, plain_weights(): pl.pallas_call(plain_kernel, out_shape=WEIGHTS, in_specs=[VMEM], out_spec...  9.2 us
    all_to_all x1, waiting for transfers between devices, same_core(): return lax.all_to_all(sent, 'vox', 0, 0, axis_index_groups=groups)  7.22 us
  transfers between devices with their start and end apart: 16, of which 9 were waited for; matrix products, arithmetic and copies ran while one was open for 0% of the time, Pallas kernels for 51%

profile of v3, /device:TPU:1, one launch (start us, length us, event | category | flops | bytes accessed | tf_op | source)
XLA Modules:
  0.0 335.2 jit_solution(4185929873544328542)
XLA Ops:
  0.0 4.1 %collective-permute-start = (bf16[1024,256]{1,0:T(8,128)(2,1)}, bf16[1024,256]{1,0:T(8,128)(2,1)S(1)}, u32[]{:S(2)}, u32[]{:S(2)}) collective-permute-start(bf16[1024,256]{1,0:T(8,128)(2,1)} %bitcast.6), channel_id=1, source_target_pairs={{0,16},{16,0},{32,48},{48,32},{64,80},{80,64},{96,112},{112,96},{1... | collective-permute-start | bytes 1572872 | tf_op jit(solution)/shard_map/ppermute | solution.py:376
  4.1 2.1 self_gram.1
  6.2 8.1 %all-to-all-start = ((f32[16,24,128]{2,1,0:T(8,128)}), f32[16,24,128]{2,1,0:T(8,128)S(1)}, u32[]{:S(2)}, u32[]{:S(2)}) async-start(f32[16,24,128]{2,1,0:T(8,128)} %self_gram.1), calls=%async_computation | async-start | bytes 393216 | tf_op jit(solution)/shard_map/all_to_all | solution.py:380
  14.4 0.0 collective-permute-done.q_ref
  14.4 1.1 cross_gram.1
  15.4 9.2 %all-to-all-done = f32[16,24,128]{2,1,0:T(8,128)S(1)} async-done(((f32[16,24,128]{2,1,0:T(8,128)}), f32[16,24,128]{2,1,0:T(8,128)S(1)}, u32[]{:S(2)}, u32[]{:S(2)}) %all-to-all-start) | async-done | bytes 196640 | tf_op jit(solution)/shard_map/all_to_all | solution.py:380
  24.6 3.4 %all-to-all-start.1 = ((f32[16,32,128]{2,1,0:T(8,128)}), f32[16,32,128]{2,1,0:T(8,128)S(1)}, u32[]{:S(2)}, u32[]{:S(2)}) async-start(f32[16,32,128]{2,1,0:T(8,128)} %cross_gram.1), calls=%async_computation.1 | async-start | bytes 524288 | tf_op jit(solution)/shard_map/all_to_all | solution.py:380
  28.1 3.6 %collective-permute-start.1 = (f32[24,128]{1,0:T(8,128)S(1)}, f32[24,128]{1,0:T(8,128)S(1)}, u32[]{:S(2)}, u32[]{:S(2)}) collective-permute-start(f32[24,128]{1,0:T(8,128)S(1)} %reduce_sum.27), channel_id=1, source_target_pairs={{0,16},{16,0},{32,48},{48,32},{64,80},{80,64},{96,112},{112,96},{1... | collective-permute-start | bytes 36872 | tf_op jit(solution)/shard_map/ppermute | solution.py:376
  31.7 7.5 %all-to-all-done.1 = f32[16,32,128]{2,1,0:T(8,128)S(1)} async-done(((f32[16,32,128]{2,1,0:T(8,128)}), f32[16,32,128]{2,1,0:T(8,128)S(1)}, u32[]{:S(2)}, u32[]{:S(2)}) %all-to-all-start.1) | async-done | bytes 262176 | tf_op jit(solution)/shard_map/all_to_all | solution.py:380
  39.3 0.0 collective-permute-done.1
  39.3 0.7 broadcast_in_dim.4
  40.1 3.4 %all-to-all-start.2 = ((f32[8,80,128]{2,1,0:T(8,128)}), f32[8,80,128]{2,1,0:T(8,128)S(1)}, u32[]{:S(2)}, u32[]{:S(2)}) async-start(f32[8,80,128]{2,1,0:T(8,128)} %broadcast_in_dim.4), calls=%async_computation.2 | async-start | bytes 655360 | tf_op jit(solution)/shard_map/all_to_all | solution.py:386
  43.5 3.7 %collective-permute-start.3 = (bf16[1024,256]{1,0:T(8,128)(2,1)S(1)}, bf16[1024,256]{1,0:T(8,128)(2,1)S(1)}, u32[]{:S(2)}, u32[]{:S(2)}) collective-permute-start(bf16[1024,256]{1,0:T(8,128)(2,1)S(1)} %bitcast.9), channel_id=1, source_target_pairs={{0,48},{16,32},{32,16},{48,0},{64,112},{80,96},{96,80},{112,64},{1... | collective-permute-start | bytes 1572872 | tf_op jit(solution)/shard_map/ppermute | solution.py:376
  47.2 2.8 collective-permute-start.4
  50.0 7.2 %all-to-all-done.2.mine_ref = f32[8,80,128]{2,1,0:T(8,128)S(1)} async-done(((f32[8,80,128]{2,1,0:T(8,128)}), f32[8,80,128]{2,1,0:T(8,128)S(1)}, u32[]{:S(2)}, u32[]{:S(2)}) %all-to-all-start.2) | async-done | bytes 327712 | tf_op jit(solution)/shard_map/all_to_all | solution.py:386
  57.2 2.3 collective-permute-start.2
  59.6 1.2 collective-permute-done.2.theirs_ref
  60.8 160.6 %full_weights.1.w_ref = bf16[2,256,256]{2,1,0:T(8,128)(2,1)S(1)} custom-call(s32[1]{0:T(128)} %bitcast.1.core_ref, f32[8,80,128]{2,1,0:T(8,128)S(1)} %all-to-all-done.2.mine_ref, f32[8,80,128]{2,1,0:T(8,128)S(1)} %collective-permute-done.2.theirs_ref), custom_call_target="tpu_custom_call" | custom-call | tf_op jit(solution)/shard_map/full_weights/pallas_call | solution.py:214
  221.4 0.0 collective-permute-done.3.r_ref.p_ref
  221.4 0.0 collective-permute-done.4.s_ref.q_ref
  221.4 2.5 project.2
  223.9 3.7 %all-to-all-start.3 = ((bf16[16,16,512]{2,1,0:T(8,128)(2,1)}), bf16[16,16,512]{2,1,0:T(8,128)(2,1)S(1)}, u32[]{:S(2)}, u32[]{:S(2)}) async-start(bf16[16,16,512]{2,1,0:T(8,128)(2,1)} %get-tuple-element.10), calls=%async_computation.3 | async-start | bytes 524288 | tf_op jit(solution)/shard_map/all_to_all | solution.py:380
  227.6 4.0 %collective-permute-start.6 = (bf16[1024,256]{1,0:T(8,128)(2,1)}, bf16[1024,256]{1,0:T(8,128)(2,1)S(1)}, u32[]{:S(2)}, u32[]{:S(2)}) collective-permute-start(bf16[1024,256]{1,0:T(8,128)(2,1)} %get-tuple-element.9.p_ref), channel_id=1, source_target_pairs={{0,64},{16,80},{32,96},{48,112},{64,0},{80,16},{96,32},{112,48},{1... | collective-permute-start | bytes 1572872 | tf_op jit(solution)/shard_map/ppermute | solution.py:376
  231.6 3.4 %collective-permute-start.7 = (bf16[1024,256]{1,0:T(8,128)(2,1)}, bf16[1024,256]{1,0:T(8,128)(2,1)S(1)}, u32[]{:S(2)}, u32[]{:S(2)}) collective-permute-start(bf16[1024,256]{1,0:T(8,128)(2,1)} %get-tuple-element.9.p_ref), channel_id=1, source_target_pairs={{0,112},{16,96},{32,80},{48,64},{64,48},{80,32},{96,16},{112,0},{1... | collective-permute-start | bytes 1572872 | tf_op jit(solution)/shard_map/ppermute | solution.py:376
  235.0 2.8 collective-permute-start.5
  237.8 7.8 %collective-permute-done.5.w_ref = bf16[2,256,256]{2,1,0:T(8,128)(2,1)S(1)} collective-permute-done((bf16[2,256,256]{2,1,0:T(8,128)(2,1)S(1)}, bf16[2,256,256]{2,1,0:T(8,128)(2,1)S(1)}, u32[]{:S(2)}, u32[]{:S(2)}) %collective-permute-start.5) | collective-permute-done | bytes 262176 | tf_op jit(solution)/shard_map/ppermute | solution.py:376
  245.6 0.0 all-to-all-done.3.parts_ref
  245.6 0.9 cross_rows.2
  246.5 19.4 %all-to-all-start.4 = ((bf16[16,16,256]{2,1,0:T(8,128)(2,1)}), bf16[16,16,256]{2,1,0:T(8,128)(2,1)S(1)}, u32[]{:S(2)}, u32[]{:S(2)}) async-start(bf16[16,16,256]{2,1,0:T(8,128)(2,1)} %cross_rows.2), calls=%async_computation.4 | async-start | bytes 262144 | tf_op jit(solution)/shard_map/all_to_all | solution.py:380
  265.9 0.5 mix.2.q_ref
  266.4 8.4 %all-to-all-done.4 = bf16[16,16,256]{2,1,0:T(8,128)(2,1)S(1)} async-done(((bf16[16,16,256]{2,1,0:T(8,128)(2,1)}), bf16[16,16,256]{2,1,0:T(8,128)(2,1)S(1)}, u32[]{:S(2)}, u32[]{:S(2)}) %all-to-all-start.4) | async-done | bytes 131104 | tf_op jit(solution)/shard_map/all_to_all | solution.py:380
  274.8 4.5 %plain_weights.2.w_ref = bf16[2,256,256]{2,1,0:T(8,128)(2,1)S(1)} custom-call(bf16[256,256]{1,0:T(8,128)(2,1)S(1)} %bitcast.12), custom_call_target="tpu_custom_call" | custom-call | tf_op jit(solution)/shard_map/plain_weights/pallas_call | solution.py:230
  279.3 0.0 collective-permute-done.7.s_ref.q_ref
  279.3 3.2 project.3
  282.5 3.4 %all-to-all-start.5 = ((bf16[16,16,512]{2,1,0:T(8,128)(2,1)}), bf16[16,16,512]{2,1,0:T(8,128)(2,1)S(1)}, u32[]{:S(2)}, u32[]{:S(2)}) async-start(bf16[16,16,512]{2,1,0:T(8,128)(2,1)} %get-tuple-element.12), calls=%async_computation.5 | async-start | bytes 524288 | tf_op jit(solution)/shard_map/all_to_all | solution.py:380
  286.0 3.4 %collective-permute-start.8 = (bf16[2,256,256]{2,1,0:T(8,128)(2,1)S(1)}, bf16[2,256,256]{2,1,0:T(8,128)(2,1)S(1)}, u32[]{:S(2)}, u32[]{:S(2)}) collective-permute-start(bf16[2,256,256]{2,1,0:T(8,128)(2,1)S(1)} %plain_weights.2.w_ref), channel_id=1, source_target_pairs={{0,64},{16,80},{32,96},{48,112},{64,0},{80,16},{96,32},{112,48},{1... | collective-permute-start | bytes 786440 | tf_op jit(solution)/shard_map/ppermute | solution.py:376
  289.4 6.4 %collective-permute-done.8.w_ref = bf16[2,256,256]{2,1,0:T(8,128)(2,1)S(1)} collective-permute-done((bf16[2,256,256]{2,1,0:T(8,128)(2,1)S(1)}, bf16[2,256,256]{2,1,0:T(8,128)(2,1)S(1)}, u32[]{:S(2)}, u32[]{:S(2)}) %collective-permute-start.8) | collective-permute-done | bytes 262176 | tf_op jit(solution)/shard_map/ppermute | solution.py:376
  295.8 1.9 all-to-all-done.5.parts_ref
  297.6 0.9 cross_rows.3
  298.6 5.6 %all-to-all-start.6 = ((bf16[16,16,256]{2,1,0:T(8,128)(2,1)}), bf16[16,16,256]{2,1,0:T(8,128)(2,1)S(1)}, u32[]{:S(2)}, u32[]{:S(2)}) async-start(bf16[16,16,256]{2,1,0:T(8,128)(2,1)} %cross_rows.3), calls=%async_computation.6 | async-start | bytes 262144 | tf_op jit(solution)/shard_map/all_to_all | solution.py:380
  304.2 0.5 mix.3.q_ref
  304.6 8.4 %all-to-all-done.6 = bf16[16,16,256]{2,1,0:T(8,128)(2,1)S(1)} async-done(((bf16[16,16,256]{2,1,0:T(8,128)(2,1)}), bf16[16,16,256]{2,1,0:T(8,128)(2,1)S(1)}, u32[]{:S(2)}, u32[]{:S(2)}) %all-to-all-start.6) | async-done | bytes 131104 | tf_op jit(solution)/shard_map/all_to_all | solution.py:380
  313.0 4.7 %plain_weights.3.w_ref = bf16[2,256,256]{2,1,0:T(8,128)(2,1)S(1)} custom-call(bf16[256,256]{1,0:T(8,128)(2,1)S(1)} %bitcast.13), custom_call_target="tpu_custom_call" | custom-call | tf_op jit(solution)/shard_map/plain_weights/pallas_call | solution.py:230
  317.8 0.0 copy-start.1
  317.8 1.2 copy-done.1
  319.0 1.3 load.1
  320.3 14.3 %all_to_all.40 = bf16[16,16,512]{2,1,0:T(8,128)(2,1)S(1)} all-to-all(bf16[16,16,512]{2,1,0:T(8,128)(2,1)S(1)} %load.1), channel_id=1, replica_groups=mesh['grp'=32,'vox'=16] {'vox'}, dimensions={0} | all-to-all | bytes 524288 | tf_op jit(solution)/shard_map/all_to_all | solution.py:380
  334.6 0.7 convert_reduce_fusion
  (6 shorter events, 0.1 us)
Async XLA Ops:
  0.0 14.4 %copy-start = (bf16[1,1024,256]{2,1,0:T(8,128)(2,1)S(1)}, bf16[1,1024,256]{2,1,0:T(8,128)(2,1)}, u32[]{:S(2)}) copy-start(bf16[1,1024,256]{2,1,0:T(8,128)(2,1)} %param.2) | copy-start | bytes 1572868
  0.0 14.4 %collective-permute-start = (bf16[1024,256]{1,0:T(8,128)(2,1)}, bf16[1024,256]{1,0:T(8,128)(2,1)S(1)}, u32[]{:S(2)}, u32[]{:S(2)}) collective-permute-start(bf16[1024,256]{1,0:T(8,128)(2,1)} %bitcast.6), channel_id=1, source_target_pairs={{0,16},{16,0},{32,48},{48,32},{64,80},{80,64},{96,112},{112,96},{1... | collective-permute-start | bytes 1572872 | tf_op jit(solution)/shard_map/ppermute | solution.py:376
  6.2 18.4 %all-to-all-start = ((f32[16,24,128]{2,1,0:T(8,128)}), f32[16,24,128]{2,1,0:T(8,128)S(1)}, u32[]{:S(2)}, u32[]{:S(2)}) async-start(f32[16,24,128]{2,1,0:T(8,128)} %self_gram.1), calls=%async_computation | async-start | bytes 393216 | tf_op jit(solution)/shard_map/all_to_all | solution.py:380
  24.6 14.6 %all-to-all-start.1 = ((f32[16,32,128]{2,1,0:T(8,128)}), f32[16,32,128]{2,1,0:T(8,128)S(1)}, u32[]{:S(2)}, u32[]{:S(2)}) async-start(f32[16,32,128]{2,1,0:T(8,128)} %cross_gram.1), calls=%async_computation.1 | async-start | bytes 524288 | tf_op jit(solution)/shard_map/all_to_all | solution.py:380
  28.1 11.2 %collective-permute-start.1 = (f32[24,128]{1,0:T(8,128)S(1)}, f32[24,128]{1,0:T(8,128)S(1)}, u32[]{:S(2)}, u32[]{:S(2)}) collective-permute-start(f32[24,128]{1,0:T(8,128)S(1)} %reduce_sum.27), channel_id=1, source_target_pairs={{0,16},{16,0},{32,48},{48,32},{64,80},{80,64},{96,112},{112,96},{1... | collective-permute-start | bytes 36872 | tf_op jit(solution)/shard_map/ppermute | solution.py:376
  40.1 17.2 %all-to-all-start.2 = ((f32[8,80,128]{2,1,0:T(8,128)}), f32[8,80,128]{2,1,0:T(8,128)S(1)}, u32[]{:S(2)}, u32[]{:S(2)}) async-start(f32[8,80,128]{2,1,0:T(8,128)} %broadcast_in_dim.4), calls=%async_computation.2 | async-start | bytes 655360 | tf_op jit(solution)/shard_map/all_to_all | solution.py:386
  43.5 177.9 %collective-permute-start.3 = (bf16[1024,256]{1,0:T(8,128)(2,1)S(1)}, bf16[1024,256]{1,0:T(8,128)(2,1)S(1)}, u32[]{:S(2)}, u32[]{:S(2)}) collective-permute-start(bf16[1024,256]{1,0:T(8,128)(2,1)S(1)} %bitcast.9), channel_id=1, source_target_pairs={{0,48},{16,32},{32,16},{48,0},{64,112},{80,96},{96,80},{112,64},{1... | collective-permute-start | bytes 1572872 | tf_op jit(solution)/shard_map/ppermute | solution.py:376
  47.2 174.2 %collective-permute-start.4 = (bf16[1024,256]{1,0:T(8,128)(2,1)S(1)}, bf16[1024,256]{1,0:T(8,128)(2,1)S(1)}, u32[]{:S(2)}, u32[]{:S(2)}) collective-permute-start(bf16[1024,256]{1,0:T(8,128)(2,1)S(1)} %collective-permute-done.q_ref), channel_id=1, source_target_pairs={{0,48},{16,32},{32,16},{48,0},{64,112},{80,96},{96,80},{112,64},{1... | collective-permute-start | bytes 1572872 | tf_op jit(solution)/shard_map/ppermute | solution.py:376
  57.2 3.6 %collective-permute-start.2 = (f32[8,80,128]{2,1,0:T(8,128)S(1)}, f32[8,80,128]{2,1,0:T(8,128)S(1)}, u32[]{:S(2)}, u32[]{:S(2)}) collective-permute-start(f32[8,80,128]{2,1,0:T(8,128)S(1)} %all-to-all-done.2.mine_ref), channel_id=1, source_target_pairs={{0,1},{1,0},{2,3},{3,2},{4,5},{5,4},{6,7},{7,6},{8,9},{9,8},{10,11... | collective-permute-start | bytes 983048 | tf_op jit(solution)/shard_map/ppermute | solution.py:390
  223.9 21.7 %all-to-all-start.3 = ((bf16[16,16,512]{2,1,0:T(8,128)(2,1)}), bf16[16,16,512]{2,1,0:T(8,128)(2,1)S(1)}, u32[]{:S(2)}, u32[]{:S(2)}) async-start(bf16[16,16,512]{2,1,0:T(8,128)(2,1)} %get-tuple-element.10), calls=%async_computation.3 | async-start | bytes 524288 | tf_op jit(solution)/shard_map/all_to_all | solution.py:380
  227.6 51.7 %collective-permute-start.6 = (bf16[1024,256]{1,0:T(8,128)(2,1)}, bf16[1024,256]{1,0:T(8,128)(2,1)S(1)}, u32[]{:S(2)}, u32[]{:S(2)}) collective-permute-start(bf16[1024,256]{1,0:T(8,128)(2,1)} %get-tuple-element.9.p_ref), channel_id=1, source_target_pairs={{0,64},{16,80},{32,96},{48,112},{64,0},{80,16},{96,32},{112,48},{1... | collective-permute-start | bytes 1572872 | tf_op jit(solution)/shard_map/ppermute | solution.py:376
  231.6 47.7 %collective-permute-start.7 = (bf16[1024,256]{1,0:T(8,128)(2,1)}, bf16[1024,256]{1,0:T(8,128)(2,1)S(1)}, u32[]{:S(2)}, u32[]{:S(2)}) collective-permute-start(bf16[1024,256]{1,0:T(8,128)(2,1)} %get-tuple-element.9.p_ref), channel_id=1, source_target_pairs={{0,112},{16,96},{32,80},{48,64},{64,48},{80,32},{96,16},{112,0},{1... | collective-permute-start | bytes 1572872 | tf_op jit(solution)/shard_map/ppermute | solution.py:376
  235.0 10.6 %collective-permute-start.5 = (bf16[2,256,256]{2,1,0:T(8,128)(2,1)S(1)}, bf16[2,256,256]{2,1,0:T(8,128)(2,1)S(1)}, u32[]{:S(2)}, u32[]{:S(2)}) collective-permute-start(bf16[2,256,256]{2,1,0:T(8,128)(2,1)S(1)} %full_weights.1.w_ref), channel_id=1, source_target_pairs={{0,48},{16,32},{32,16},{48,0},{64,112},{80,96},{96,80},{112,64},{1... | collective-permute-start | bytes 786440 | tf_op jit(solution)/shard_map/ppermute | solution.py:376
  246.5 28.3 %all-to-all-start.4 = ((bf16[16,16,256]{2,1,0:T(8,128)(2,1)}), bf16[16,16,256]{2,1,0:T(8,128)(2,1)S(1)}, u32[]{:S(2)}, u32[]{:S(2)}) async-start(bf16[16,16,256]{2,1,0:T(8,128)(2,1)} %cross_rows.2), calls=%async_computation.4 | async-start | bytes 262144 | tf_op jit(solution)/shard_map/all_to_all | solution.py:380
  282.5 15.1 %all-to-all-start.5 = ((bf16[16,16,512]{2,1,0:T(8,128)(2,1)}), bf16[16,16,512]{2,1,0:T(8,128)(2,1)S(1)}, u32[]{:S(2)}, u32[]{:S(2)}) async-start(bf16[16,16,512]{2,1,0:T(8,128)(2,1)} %get-tuple-element.12), calls=%async_computation.5 | async-start | bytes 524288 | tf_op jit(solution)/shard_map/all_to_all | solution.py:380
  286.0 9.8 %collective-permute-start.8 = (bf16[2,256,256]{2,1,0:T(8,128)(2,1)S(1)}, bf16[2,256,256]{2,1,0:T(8,128)(2,1)S(1)}, u32[]{:S(2)}, u32[]{:S(2)}) collective-permute-start(bf16[2,256,256]{2,1,0:T(8,128)(2,1)S(1)} %plain_weights.2.w_ref), channel_id=1, source_target_pairs={{0,64},{16,80},{32,96},{48,112},{64,0},{80,16},{96,32},{112,48},{1... | collective-permute-start | bytes 786440 | tf_op jit(solution)/shard_map/ppermute | solution.py:376
  298.6 14.5 %all-to-all-start.6 = ((bf16[16,16,256]{2,1,0:T(8,128)(2,1)}), bf16[16,16,256]{2,1,0:T(8,128)(2,1)S(1)}, u32[]{:S(2)}, u32[]{:S(2)}) async-start(bf16[16,16,256]{2,1,0:T(8,128)(2,1)} %cross_rows.3), calls=%async_computation.6 | async-start | bytes 262144 | tf_op jit(solution)/shard_map/all_to_all | solution.py:380
  317.8 1.2 copy-start.1

commit v4 on v3

--- a/solution.py
+++ b/solution.py
@@ -58,7 +58,7 @@
     return col, row
 
 
-def inverse_factor(m):
+def inverse_factor(m, steps):
     r, c = iotas()
     eye = r == c
     below = r > c
@@ -69,7 +69,7 @@
     s2 = dot1(s, s, NN)
     t = one - s
     x = t + dot1(t, s2, NN)
-    for _ in range(2):
+    for _ in range(steps):
         mk = dot1(dot1(x, m, NN), x, NT)
         col, row = inv_sqrt_diag(mk, eye)
         s = jnp.where(below, col * mk * row, 0.0)
@@ -153,11 +153,11 @@
     v0, v1 = times(u0, u1)
     us0, us1 = split(u0), split(u1)
     m = dot3(split(v0), us0, NT) + dot3(split(v1), us1, NT)
-    x, size = inverse_factor(m)
+    x, size = inverse_factor(m, 1 if plain else 2)
     xs = split(x)
     out_ref[0] = (dot3(xs, us0, NN) * unscale).astype(BF16)
     out_ref[1] = (dot3(xs, us1, NN) * unscale).astype(BF16)
-    good = jnp.where(size < 0.01, 1, 0)
+    good = jnp.where(size < 0.06, 1, 0)
 
     @pl.when(good == 0)
     def _():
@@ -187,11 +187,23 @@
         out_ref[1] = (y_ref[1] * unscale).astype(BF16)
 
 
+def mixed(p_ref, q_ref, w_ref):
+    out = dot1(p_ref[...], w_ref[0], NT) + dot1(q_ref[...], w_ref[1], NT)
+    return out.astype(BF16)
+
+
+def project_into(node, sides, proj_ref):
+    for k, side in enumerate(sides):
+        got = dot1(node, side[...], TN).astype(BF16)
+        proj_ref[:, :, N * k : N * (k + 1)] = got.reshape(VOX, ROWS, N)
+
+
 SCRATCH = [pltpu.VMEM((2, N, N), F32)] * 2 + [pltpu.VMEM((N, N), F32)] * 2
 WEIGHTS = jax.ShapeDtypeStruct((2, N, N), BF16)
 
 
-def full_kernel(core_ref, mine_ref, theirs_ref, out_ref, a_ref, c_ref, *scratch):
+def full_kernel(core_ref, mine_ref, theirs_ref, p_ref, q_ref, r_ref, s_ref, *refs):
+    out_ref, node_hbm, proj_ref, a_ref, c_ref, node_ref, sem = refs[:7]
     core = core_ref[0]
     for half, ref in ((core, mine_ref), (1 - core, theirs_ref)):
         for y in range(8):
@@ -207,19 +219,32 @@
             c_ref[at, H:] = ref[y, 64:80, :]
     for k in range(2):
         a_ref[k, :H, H:] = a_ref[k, H:, :H].T
-    weights_body(a_ref[0], a_ref[1], c_ref[...], out_ref, *scratch)
-
-
-def full_weights(core, mine, theirs):
+    weights_body(a_ref[0], a_ref[1], c_ref[...], out_ref, *refs[7:])
+    node = mixed(p_ref, q_ref, out_ref)
+    node_ref[...] = node
+    copy = pltpu.make_async_copy(node_ref, node_hbm, sem)
+    copy.start()
+    project_into(node, (r_ref, s_ref), proj_ref)
+    copy.wait()
+
+
+def projections(node):
+    parts = jax.ShapeDtypeStruct((VOX, ROWS, 2 * N), BF16)
+    return jax.ShapeDtypeStruct(node.shape, BF16), parts
+
+
+def full_merge(core, mine, theirs, p, q, r, s):
     return pl.pallas_call(
         full_kernel,
-        out_shape=WEIGHTS,
-        in_specs=[SMEM, VMEM, VMEM],
-        out_specs=VMEM,
-        scratch_shapes=[pltpu.VMEM((2, N, N), F32), pltpu.VMEM((N, N), F32)] + SCRATCH,
-        compiler_params=params(12),
-        name="full_weights",
-    )(core, mine, theirs)
+        out_shape=(WEIGHTS,) + projections(p),
+        in_specs=[SMEM] + [VMEM] * 6,
+        out_specs=(VMEM, HBM, VMEM),
+        scratch_shapes=[pltpu.VMEM((2, N, N), F32), pltpu.VMEM((N, N), F32)]
+        + [pltpu.VMEM(p.shape, BF16), pltpu.SemaphoreType.DMA]
+        + SCRATCH,
+        compiler_params=params(16),
+        name="full_merge",
+    )(core, mine, theirs, p, q, r, s)
 
 
 def plain_kernel(cross_ref, out_ref, *scratch):
@@ -239,8 +264,7 @@
 
 
 def mix_kernel(p_ref, q_ref, w_ref, out_ref):
-    out = dot1(p_ref[...], w_ref[0], NT) + dot1(q_ref[...], w_ref[1], NT)
-    out_ref[...] = out.astype(BF16)
+    out_ref[...] = mixed(p_ref, q_ref, w_ref)
 
 
 def mix(p, q, w):
@@ -255,24 +279,18 @@
 
 
 def project_kernel(p_ref, q_ref, w_ref, r_ref, s_ref, out_hbm, proj_ref, out_ref, sem):
-    out = dot1(p_ref[...], w_ref[0], NT) + dot1(q_ref[...], w_ref[1], NT)
-    out = out.astype(BF16)
+    out = mixed(p_ref, q_ref, w_ref)
     out_ref[...] = out
     copy = pltpu.make_async_copy(out_ref, out_hbm, sem)
     copy.start()
-    for k, side in enumerate((r_ref, s_ref)):
-        got = dot1(out, side[...], TN).astype(BF16)
-        proj_ref[:, :, N * k : N * (k + 1)] = got.reshape(VOX, ROWS, N)
+    project_into(out, (r_ref, s_ref), proj_ref)
     copy.wait()
 
 
 def project(p, q, w, r, s):
     return pl.pallas_call(
         project_kernel,
-        out_shape=(
-            jax.ShapeDtypeStruct(p.shape, BF16),
-            jax.ShapeDtypeStruct((VOX, ROWS, 2 * N), BF16),
-        ),
+        out_shape=projections(p),
         in_specs=[VMEM] * 5,
         out_specs=(HBM, VMEM),
         scratch_shapes=[pltpu.VMEM(p.shape, BF16), pltpu.SemaphoreType.DMA],
@@ -281,26 +299,32 @@
     )(p, q, w, r, s)
 
 
-def load_kernel(p_hbm, q_ref, w_ref, series_ref, out_ref, p_ref, sem):
-    copy = pltpu.make_async_copy(p_hbm, p_ref, sem)
-    copy.start()
-    root = dot1(q_ref[...], w_ref[1], NT)
-    copy.wait()
-    root = (root + dot1(p_ref[...], w_ref[0], NT)).astype(BF16)
-    got = dot1(root, series_ref[...], TN).astype(BF16)
-    out_ref[...] = got.reshape(out_ref.shape)
-
-
-def load(p, q, w, series):
-    return pl.pallas_call(
-        load_kernel,
+def last_kernel(cross_ref, p_hbm, q_ref, series_hbm, out_ref, *refs):
+    p_ref, series_ref, p_sem, series_sem, w_ref = refs[:5]
+    first = pltpu.make_async_copy(p_hbm, p_ref, p_sem)
+    first.start()
+    second = pltpu.make_async_copy(series_hbm, series_ref, series_sem)
+    second.start()
+    weights_body(None, None, cross_ref[...].astype(F32), w_ref, *refs[5:])
+    first.wait()
+    second.wait()
+    root = mixed(p_ref, q_ref, w_ref)
+    out_ref[...] = dot1(root, series_ref[...], TN).astype(BF16).reshape(out_ref.shape)
+
+
+def last_merge(cross, p, q, series):
+    return pl.pallas_call(
+        last_kernel,
         out_shape=jax.ShapeDtypeStruct((VOX, ROWS, series.shape[1]), BF16),
-        in_specs=[HBM, VMEM, VMEM, VMEM],
-        out_specs=VMEM,
-        scratch_shapes=[pltpu.VMEM(p.shape, BF16), pltpu.SemaphoreType.DMA],
-        compiler_params=params(8),
-        name="load",
-    )(p, q, w, series)
+        in_specs=[VMEM, HBM, VMEM, HBM],
+        out_specs=VMEM,
+        scratch_shapes=[pltpu.VMEM(p.shape, BF16), pltpu.VMEM(series.shape, BF16)]
+        + [pltpu.SemaphoreType.DMA] * 2
+        + [pltpu.VMEM((2, N, N), BF16)]
+        + SCRATCH,
+        compiler_params=params(16),
+        name="last_merge",
+    )(cross, p, q, pltpu.with_memory_space_constraint(series, pltpu.MemorySpace.HBM))
 
 
 def self_gram_kernel(p_hbm, out_ref, p_ref, sems):
@@ -405,9 +429,7 @@
     rows = jnp.concatenate([own_rows, other_rows, cross_rows], axis=0)
     mine = same_core(rows)
     theirs = swap_cores(mine)
-    w = full_weights(core, mine, theirs)
-
-    left, parts = project(own, other, w, far_own, far_other)
+    w, left, parts = full_merge(core, mine, theirs, own, other, far_own, far_other)
     parts = exchange(parts)
     far_w = partner(w, 3)
     deep_left = partner(left, 4)
@@ -421,9 +443,7 @@
     deep_w = partner(w, 4)
     cross = exchange(cross_rows_of(parts, deep_w))
     right = mix(deep_left, deep_right, deep_w)
-    w = plain_weights(cross.reshape(N, N))
-
-    parts = load(left, right, w, series)
+    parts = last_merge(cross.reshape(N, N), left, right, series)
     return add_up(exchange(parts))
 
 

time: 336 us -> 348 us (1.036)
  waiting for transfers between devices: 58.1 us -> 80.1 us
  starting transfers between devices: 77.2 us -> 69.8 us
    ppermute x8, waiting for transfers between devices: 14.2 us -> 37.5 us  [partner(): return lax.ppermute(value, 'grp', [(g, g ^ mask) for g in range(GRP)])]
    all_to_all x6, starting transfers between devices: 43.7 us -> 36.3 us  [exchange(): return lax.all_to_all(parts, 'vox', 0, 0)]
    pallas_call x2 -> x1, Pallas kernels: 9.2 us -> 3.67 us  [plain_weights(): pl.pallas_call(plain_kernel, out_shape=WEIGHTS, in_specs=[VMEM], out_spec...]
    pallas_call x4 -> x3, Pallas kernels: 168 us -> 170 us  [the longest x1 163 us: full_merge(): pl.pallas_call(full_kernel, out_shape=(WEIGHTS,) + projections(p), in_spe...]
  transfers between devices with their start and end apart: 16 -> 16, of which waited for: 9 -> 10; matrix products, arithmetic and copies ran while one was open for 0% -> 0% of each run, Pallas kernels for 51% -> 3%
where the time goes in v4:
time: 348 us; the launch traced here: 346 us
  Pallas kernels  180 us (52%)
  waiting for transfers between devices  80.1 us (23%)
  starting transfers between devices  69.8 us (20%)
  blocking collectives  14.3 us (4%)
    pallas_call x1, Pallas kernels, full_merge(): pl.pallas_call(full_kernel, out_shape=(WEIGHTS,) + projections(p), in_spe...  163 us
    ppermute x8, waiting for transfers between devices, partner(): return lax.ppermute(value, 'grp', [(g, g ^ mask) for g in range(GRP)])  37.5 us
    all_to_all x6, starting transfers between devices, exchange(): return lax.all_to_all(parts, 'vox', 0, 0)  36.3 us
    all_to_all x6, waiting for transfers between devices, exchange(): return lax.all_to_all(parts, 'vox', 0, 0)  35.4 us
    ppermute x8, starting transfers between devices, partner(): return lax.ppermute(value, 'grp', [(g, g ^ mask) for g in range(GRP)])  27.7 us
    all_to_all x1, blocking collectives, exchange(): return lax.all_to_all(parts, 'vox', 0, 0)  14.3 us
    all_to_all x1, waiting for transfers between devices, same_core(): return lax.all_to_all(sent, 'vox', 0, 0, axis_index_groups=groups)  7.22 us
  transfers between devices with their start and end apart: 16, of which 10 were waited for; matrix products, arithmetic and copies ran while one was open for 0% of the time, Pallas kernels for 3%

profile of v4, /device:TPU:1, one launch (start us, length us, event | category | flops | bytes accessed | tf_op | source)
XLA Modules:
  0.0 346.3 jit_solution(11437856204099924322)
XLA Ops:
  0.0 4.1 %collective-permute-start.1 = (bf16[1024,256]{1,0:T(8,128)(2,1)}, bf16[1024,256]{1,0:T(8,128)(2,1)S(1)}, u32[]{:S(2)}, u32[]{:S(2)}) collective-permute-start(bf16[1024,256]{1,0:T(8,128)(2,1)} %bitcast.6), channel_id=1, source_target_pairs={{0,16},{16,0},{32,48},{48,32},{64,80},{80,64},{96,112},{112,96},{1... | collective-permute-start | bytes 1572872 | tf_op jit(solution)/shard_map/ppermute | solution.py:400
  4.1 2.1 self_gram.1
  6.2 8.1 %all-to-all-start = ((f32[16,24,128]{2,1,0:T(8,128)}), f32[16,24,128]{2,1,0:T(8,128)S(1)}, u32[]{:S(2)}, u32[]{:S(2)}) async-start(f32[16,24,128]{2,1,0:T(8,128)} %self_gram.1), calls=%async_computation | async-start | bytes 393216 | tf_op jit(solution)/shard_map/all_to_all | solution.py:404
  14.4 0.0 collective-permute-done.1.q_ref
  14.4 0.0 copy-done
  14.4 1.1 cross_gram.1
  15.4 9.2 %all-to-all-done = f32[16,24,128]{2,1,0:T(8,128)S(1)} async-done(((f32[16,24,128]{2,1,0:T(8,128)}), f32[16,24,128]{2,1,0:T(8,128)S(1)}, u32[]{:S(2)}, u32[]{:S(2)}) %all-to-all-start) | async-done | bytes 196640 | tf_op jit(solution)/shard_map/all_to_all | solution.py:404
  24.6 3.4 all-to-all-start.1
  28.1 3.6 %collective-permute-start = (f32[24,128]{1,0:T(8,128)S(1)}, f32[24,128]{1,0:T(8,128)S(1)}, u32[]{:S(2)}, u32[]{:S(2)}) collective-permute-start(f32[24,128]{1,0:T(8,128)S(1)} %reduce_sum.27), channel_id=1, source_target_pairs={{0,16},{16,0},{32,48},{48,32},{64,80},{80,64},{96,112},{112,96},{1... | collective-permute-start | bytes 36872 | tf_op jit(solution)/shard_map/ppermute | solution.py:400
  31.7 7.5 %all-to-all-done.1 = f32[16,32,128]{2,1,0:T(8,128)S(1)} async-done(((f32[16,32,128]{2,1,0:T(8,128)}), f32[16,32,128]{2,1,0:T(8,128)S(1)}, u32[]{:S(2)}, u32[]{:S(2)}) %all-to-all-start.1) | async-done | bytes 262176 | tf_op jit(solution)/shard_map/all_to_all | solution.py:404
  39.3 0.0 collective-permute-done
  39.3 0.7 broadcast_in_dim.4
  40.1 3.4 all-to-all-start.2
  43.5 3.7 %collective-permute-start.3 = (bf16[1024,256]{1,0:T(8,128)(2,1)S(1)}, bf16[1024,256]{1,0:T(8,128)(2,1)S(1)}, u32[]{:S(2)}, u32[]{:S(2)}) collective-permute-start(bf16[1024,256]{1,0:T(8,128)(2,1)S(1)} %bitcast.9), channel_id=1, source_target_pairs={{0,48},{16,32},{32,16},{48,0},{64,112},{80,96},{96,80},{112,64},{1... | collective-permute-start | bytes 1572872 | tf_op jit(solution)/shard_map/ppermute | solution.py:400
  47.2 2.8 collective-permute-start.4
  50.0 7.2 %all-to-all-done.2.mine_ref = f32[8,80,128]{2,1,0:T(8,128)S(1)} async-done(((f32[8,80,128]{2,1,0:T(8,128)}), f32[8,80,128]{2,1,0:T(8,128)S(1)}, u32[]{:S(2)}, u32[]{:S(2)}) %all-to-all-start.2) | async-done | bytes 327712 | tf_op jit(solution)/shard_map/all_to_all | solution.py:410
  57.2 2.3 collective-permute-start.2
  59.6 0.5 collective-permute-done.3.r_ref.p_ref
  60.1 11.2 %collective-permute-done.4.s_ref.q_ref = bf16[1024,256]{1,0:T(8,128)(2,1)S(1)} collective-permute-done((bf16[1024,256]{1,0:T(8,128)(2,1)S(1)}, bf16[1024,256]{1,0:T(8,128)(2,1)S(1)}, u32[]{:S(2)}, u32[]{:S(2)}) %collective-permute-start.4) | collective-permute-done | bytes 524320 | tf_op jit(solution)/shard_map/ppermute | solution.py:400
  71.3 0.0 collective-permute-done.2.theirs_ref
  71.3 162.8 %full_merge.1 = (bf16[2,256,256]{2,1,0:T(8,128)(2,1)S(1)}, bf16[1024,256]{1,0:T(8,128)(2,1)S(1)}, bf16[16,16,512]{2,1,0:T(8,128)(2,1)}) custom-call(s32[1]{0:T(128)} %bitcast.core_ref, f32[8,80,128]{2,1,0:T(8,128)S(1)} %all-to-all-done.2.mine_ref, f32[8,80,128]{2,1,0:T(8,128)S(1)} %collective-permute-done.2.theirs_ref, bf16[1024,256]{1,0:T(8,128)(2,1)S(1)} %bitcast.10, ...), custom_call_target="tpu_custom_call" | custom-call | tf_op jit(solution)/shard_map/full_merge/pallas_call | solution.py:237
  234.1 0.0 copy-start.1
  234.1 0.7 copy-done.1
  234.8 7.7 %all-to-all-start.3 = ((bf16[16,16,512]{2,1,0:T(8,128)(2,1)}), bf16[16,16,512]{2,1,0:T(8,128)(2,1)S(1)}, u32[]{:S(2)}, u32[]{:S(2)}) async-start(bf16[16,16,512]{2,1,0:T(8,128)(2,1)} %get-tuple-element.12), calls=%async_computation.3 | async-start | bytes 524288 | tf_op jit(solution)/shard_map/all_to_all | solution.py:404
  242.5 4.0 %collective-permute-start.6 = (bf16[1024,256]{1,0:T(8,128)(2,1)S(1)}, bf16[1024,256]{1,0:T(8,128)(2,1)S(1)}, u32[]{:S(2)}, u32[]{:S(2)}) collective-permute-start(bf16[1024,256]{1,0:T(8,128)(2,1)S(1)} %get-tuple-element.10.p_ref), channel_id=1, source_target_pairs={{0,64},{16,80},{32,96},{48,112},{64,0},{80,16},{96,32},{112,48},{1... | collective-permute-start | bytes 1572872 | tf_op jit(solution)/shard_map/ppermute | solution.py:400
  246.4 3.5 collective-permute-start.7
  249.9 2.8 collective-permute-start.5
  252.7 19.2 %collective-permute-done.5.w_ref = bf16[2,256,256]{2,1,0:T(8,128)(2,1)S(1)} collective-permute-done((bf16[2,256,256]{2,1,0:T(8,128)(2,1)}, bf16[2,256,256]{2,1,0:T(8,128)(2,1)S(1)}, u32[]{:S(2)}, u32[]{:S(2)}) %collective-permute-start.5) | collective-permute-done | bytes 262176 | tf_op jit(solution)/shard_map/ppermute | solution.py:400
  271.9 0.0 all-to-all-done.3.parts_ref
  271.9 0.9 cross_rows.2
  272.9 8.1 %all-to-all-start.4 = ((bf16[16,16,256]{2,1,0:T(8,128)(2,1)}), bf16[16,16,256]{2,1,0:T(8,128)(2,1)S(1)}, u32[]{:S(2)}, u32[]{:S(2)}) async-start(bf16[16,16,256]{2,1,0:T(8,128)(2,1)} %cross_rows.2), calls=%async_computation.4 | async-start | bytes 262144 | tf_op jit(solution)/shard_map/all_to_all | solution.py:404
  280.9 0.5 mix.2.q_ref
  281.4 8.4 %all-to-all-done.4 = bf16[16,16,256]{2,1,0:T(8,128)(2,1)S(1)} async-done(((bf16[16,16,256]{2,1,0:T(8,128)(2,1)}), bf16[16,16,256]{2,1,0:T(8,128)(2,1)S(1)}, u32[]{:S(2)}, u32[]{:S(2)}) %all-to-all-start.4) | async-done | bytes 131104 | tf_op jit(solution)/shard_map/all_to_all | solution.py:404
  289.8 3.7 %plain_weights.1.w_ref = bf16[2,256,256]{2,1,0:T(8,128)(2,1)S(1)} custom-call(bf16[256,256]{1,0:T(8,128)(2,1)S(1)} %bitcast.12), custom_call_target="tpu_custom_call" | custom-call | tf_op jit(solution)/shard_map/plain_weights/pallas_call | solution.py:255
  293.5 0.0 collective-permute-done.6.r_ref.p_ref
  293.5 0.0 collective-permute-done.7.s_ref.q_ref
  293.5 2.2 project.1
  295.7 3.4 all-to-all-start.5
  299.2 3.4 collective-permute-start.8
  302.6 6.4 %collective-permute-done.8.w_ref = bf16[2,256,256]{2,1,0:T(8,128)(2,1)S(1)} collective-permute-done((bf16[2,256,256]{2,1,0:T(8,128)(2,1)S(1)}, bf16[2,256,256]{2,1,0:T(8,128)(2,1)S(1)}, u32[]{:S(2)}, u32[]{:S(2)}) %collective-permute-start.8) | collective-permute-done | bytes 262176 | tf_op jit(solution)/shard_map/ppermute | solution.py:400
  309.0 1.9 all-to-all-done.5.parts_ref
  310.8 0.9 cross_rows.3
  311.8 5.6 %all-to-all-start.6 = ((bf16[16,16,256]{2,1,0:T(8,128)(2,1)}), bf16[16,16,256]{2,1,0:T(8,128)(2,1)S(1)}, u32[]{:S(2)}, u32[]{:S(2)}) async-start(bf16[16,16,256]{2,1,0:T(8,128)(2,1)} %cross_rows.3), calls=%async_computation.6 | async-start | bytes 262144 | tf_op jit(solution)/shard_map/all_to_all | solution.py:404
  317.4 0.5 mix.3.q_ref
  317.8 8.4 %all-to-all-done.6 = bf16[16,16,256]{2,1,0:T(8,128)(2,1)S(1)} async-done(((bf16[16,16,256]{2,1,0:T(8,128)(2,1)}), bf16[16,16,256]{2,1,0:T(8,128)(2,1)S(1)}, u32[]{:S(2)}, u32[]{:S(2)}) %all-to-all-start.6) | async-done | bytes 131104 | tf_op jit(solution)/shard_map/all_to_all | solution.py:404
  326.2 5.2 %last_merge.1 = bf16[16,16,512]{2,1,0:T(8,128)(2,1)S(1)} custom-call(bf16[256,256]{1,0:T(8,128)(2,1)S(1)} %bitcast.11, bf16[1024,256]{1,0:T(8,128)(2,1)S(1)} %get-tuple-element.14.p_hbm, bf16[1024,256]{1,0:T(8,128)(2,1)S(1)} %mix.3.q_ref, bf16[1024,512]{1,0:T(8,128)(2,1)} %bitcast.13), custom_call_target="tpu_custom_call" | custom-call | tf_op jit(solution)/shard_map/last_merge/pallas_call | solution.py:316
  331.4 14.3 %all_to_all.40 = bf16[16,16,512]{2,1,0:T(8,128)(2,1)S(1)} all-to-all(bf16[16,16,512]{2,1,0:T(8,128)(2,1)S(1)} %last_merge.1), channel_id=1, replica_groups=mesh['grp'=32,'vox'=16] {'vox'}, dimensions={0} | all-to-all | bytes 524288 | tf_op jit(solution)/shard_map/all_to_all | solution.py:404
  345.7 0.7 convert_reduce_fusion
  (4 shorter events, 0.1 us)
Async XLA Ops:
  0.0 14.4 %copy-start = (bf16[1,1024,256]{2,1,0:T(8,128)(2,1)S(1)}, bf16[1,1024,256]{2,1,0:T(8,128)(2,1)}, u32[]{:S(2)}) copy-start(bf16[1,1024,256]{2,1,0:T(8,128)(2,1)} %param.2) | copy-start | bytes 1572868
  0.0 14.4 %collective-permute-start.1 = (bf16[1024,256]{1,0:T(8,128)(2,1)}, bf16[1024,256]{1,0:T(8,128)(2,1)S(1)}, u32[]{:S(2)}, u32[]{:S(2)}) collective-permute-start(bf16[1024,256]{1,0:T(8,128)(2,1)} %bitcast.6), channel_id=1, source_target_pairs={{0,16},{16,0},{32,48},{48,32},{64,80},{80,64},{96,112},{112,96},{1... | collective-permute-start | bytes 1572872 | tf_op jit(solution)/shard_map/ppermute | solution.py:400
  6.2 18.4 %all-to-all-start = ((f32[16,24,128]{2,1,0:T(8,128)}), f32[16,24,128]{2,1,0:T(8,128)S(1)}, u32[]{:S(2)}, u32[]{:S(2)}) async-start(f32[16,24,128]{2,1,0:T(8,128)} %self_gram.1), calls=%async_computation | async-start | bytes 393216 | tf_op jit(solution)/shard_map/all_to_all | solution.py:404
  24.6 14.6 %all-to-all-start.1 = ((f32[16,32,128]{2,1,0:T(8,128)}), f32[16,32,128]{2,1,0:T(8,128)S(1)}, u32[]{:S(2)}, u32[]{:S(2)}) async-start(f32[16,32,128]{2,1,0:T(8,128)} %cross_gram.1), calls=%async_computation.1 | async-start | bytes 524288 | tf_op jit(solution)/shard_map/all_to_all | solution.py:404
  28.1 11.2 %collective-permute-start = (f32[24,128]{1,0:T(8,128)S(1)}, f32[24,128]{1,0:T(8,128)S(1)}, u32[]{:S(2)}, u32[]{:S(2)}) collective-permute-start(f32[24,128]{1,0:T(8,128)S(1)} %reduce_sum.27), channel_id=1, source_target_pairs={{0,16},{16,0},{32,48},{48,32},{64,80},{80,64},{96,112},{112,96},{1... | collective-permute-start | bytes 36872 | tf_op jit(solution)/shard_map/ppermute | solution.py:400
  40.1 17.2 %all-to-all-start.2 = ((f32[8,80,128]{2,1,0:T(8,128)}), f32[8,80,128]{2,1,0:T(8,128)S(1)}, u32[]{:S(2)}, u32[]{:S(2)}) async-start(f32[8,80,128]{2,1,0:T(8,128)} %broadcast_in_dim.4), calls=%async_computation.2 | async-start | bytes 655360 | tf_op jit(solution)/shard_map/all_to_all | solution.py:410
  43.5 16.6 %collective-permute-start.3 = (bf16[1024,256]{1,0:T(8,128)(2,1)S(1)}, bf16[1024,256]{1,0:T(8,128)(2,1)S(1)}, u32[]{:S(2)}, u32[]{:S(2)}) collective-permute-start(bf16[1024,256]{1,0:T(8,128)(2,1)S(1)} %bitcast.9), channel_id=1, source_target_pairs={{0,48},{16,32},{32,16},{48,0},{64,112},{80,96},{96,80},{112,64},{1... | collective-permute-start | bytes 1572872 | tf_op jit(solution)/shard_map/ppermute | solution.py:400
  47.2 24.2 %collective-permute-start.4 = (bf16[1024,256]{1,0:T(8,128)(2,1)S(1)}, bf16[1024,256]{1,0:T(8,128)(2,1)S(1)}, u32[]{:S(2)}, u32[]{:S(2)}) collective-permute-start(bf16[1024,256]{1,0:T(8,128)(2,1)S(1)} %collective-permute-done.1.q_ref), channel_id=1, source_target_pairs={{0,48},{16,32},{32,16},{48,0},{64,112},{80,96},{96,80},{112,64},{1... | collective-permute-start | bytes 1572872 | tf_op jit(solution)/shard_map/ppermute | solution.py:400
  57.2 14.1 %collective-permute-start.2 = (f32[8,80,128]{2,1,0:T(8,128)S(1)}, f32[8,80,128]{2,1,0:T(8,128)S(1)}, u32[]{:S(2)}, u32[]{:S(2)}) collective-permute-start(f32[8,80,128]{2,1,0:T(8,128)S(1)} %all-to-all-done.2.mine_ref), channel_id=1, source_target_pairs={{0,1},{1,0},{2,3},{3,2},{4,5},{5,4},{6,7},{7,6},{8,9},{9,8},{10,11... | collective-permute-start | bytes 983048 | tf_op jit(solution)/shard_map/ppermute | solution.py:414
  234.1 0.7 copy-start.1
  234.8 37.1 %all-to-all-start.3 = ((bf16[16,16,512]{2,1,0:T(8,128)(2,1)}), bf16[16,16,512]{2,1,0:T(8,128)(2,1)S(1)}, u32[]{:S(2)}, u32[]{:S(2)}) async-start(bf16[16,16,512]{2,1,0:T(8,128)(2,1)} %get-tuple-element.12), calls=%async_computation.3 | async-start | bytes 524288 | tf_op jit(solution)/shard_map/all_to_all | solution.py:404
  242.5 51.0 %collective-permute-start.6 = (bf16[1024,256]{1,0:T(8,128)(2,1)S(1)}, bf16[1024,256]{1,0:T(8,128)(2,1)S(1)}, u32[]{:S(2)}, u32[]{:S(2)}) collective-permute-start(bf16[1024,256]{1,0:T(8,128)(2,1)S(1)} %get-tuple-element.10.p_ref), channel_id=1, source_target_pairs={{0,64},{16,80},{32,96},{48,112},{64,0},{80,16},{96,32},{112,48},{1... | collective-permute-start | bytes 1572872 | tf_op jit(solution)/shard_map/ppermute | solution.py:400
  246.4 47.1 %collective-permute-start.7 = (bf16[1024,256]{1,0:T(8,128)(2,1)S(1)}, bf16[1024,256]{1,0:T(8,128)(2,1)S(1)}, u32[]{:S(2)}, u32[]{:S(2)}) collective-permute-start(bf16[1024,256]{1,0:T(8,128)(2,1)S(1)} %get-tuple-element.10.p_ref), channel_id=1, source_target_pairs={{0,112},{16,96},{32,80},{48,64},{64,48},{80,32},{96,16},{112,0},{1... | collective-permute-start | bytes 1572872 | tf_op jit(solution)/shard_map/ppermute | solution.py:400
  249.9 22.0 %collective-permute-start.5 = (bf16[2,256,256]{2,1,0:T(8,128)(2,1)}, bf16[2,256,256]{2,1,0:T(8,128)(2,1)S(1)}, u32[]{:S(2)}, u32[]{:S(2)}) collective-permute-start(bf16[2,256,256]{2,1,0:T(8,128)(2,1)} %copy-done.1), channel_id=1, source_target_pairs={{0,48},{16,32},{32,16},{48,0},{64,112},{80,96},{96,80},{112,64},{1... | collective-permute-start | bytes 786440 | tf_op jit(solution)/shard_map/ppermute | solution.py:400
  272.9 17.0 %all-to-all-start.4 = ((bf16[16,16,256]{2,1,0:T(8,128)(2,1)}), bf16[16,16,256]{2,1,0:T(8,128)(2,1)S(1)}, u32[]{:S(2)}, u32[]{:S(2)}) async-start(bf16[16,16,256]{2,1,0:T(8,128)(2,1)} %cross_rows.2), calls=%async_computation.4 | async-start | bytes 262144 | tf_op jit(solution)/shard_map/all_to_all | solution.py:404
  295.7 15.1 %all-to-all-start.5 = ((bf16[16,16,512]{2,1,0:T(8,128)(2,1)}), bf16[16,16,512]{2,1,0:T(8,128)(2,1)S(1)}, u32[]{:S(2)}, u32[]{:S(2)}) async-start(bf16[16,16,512]{2,1,0:T(8,128)(2,1)} %get-tuple-element.13), calls=%async_computation.5 | async-start | bytes 524288 | tf_op jit(solution)/shard_map/all_to_all | solution.py:404
  299.2 9.8 %collective-permute-start.8 = (bf16[2,256,256]{2,1,0:T(8,128)(2,1)S(1)}, bf16[2,256,256]{2,1,0:T(8,128)(2,1)S(1)}, u32[]{:S(2)}, u32[]{:S(2)}) collective-permute-start(bf16[2,256,256]{2,1,0:T(8,128)(2,1)S(1)} %plain_weights.1.w_ref), channel_id=1, source_target_pairs={{0,64},{16,80},{32,96},{48,112},{64,0},{80,16},{96,32},{112,48},{1... | collective-permute-start | bytes 786440 | tf_op jit(solution)/shard_map/ppermute | solution.py:400
  311.8 14.5 %all-to-all-start.6 = ((bf16[16,16,256]{2,1,0:T(8,128)(2,1)}), bf16[16,16,256]{2,1,0:T(8,128)(2,1)S(1)}, u32[]{:S(2)}, u32[]{:S(2)}) async-start(bf16[16,16,256]{2,1,0:T(8,128)(2,1)} %cross_rows.3), calls=%async_computation.6 | async-start | bytes 262144 | tf_op jit(solution)/shard_map/all_to_all | solution.py:404

commit v5 on v4

--- a/solution.py
+++ b/solution.py
@@ -192,10 +192,24 @@
     return out.astype(BF16)
 
 
-def project_into(node, sides, proj_ref):
+def send_out(node, sides, node_hbm, proj_hbm, node_ref, proj_ref, sems):
+    node_ref[...] = node
+    copies = [pltpu.make_async_copy(node_ref, node_hbm, sems.at[0])]
+    copies[0].start()
     for k, side in enumerate(sides):
         got = dot1(node, side[...], TN).astype(BF16)
+        at = pl.ds(N * k, N)
         proj_ref[:, :, N * k : N * (k + 1)] = got.reshape(VOX, ROWS, N)
+        copy = pltpu.make_async_copy(proj_ref.at[:, :, at], proj_hbm.at[:, :, at], sems.at[1 + k])
+        copy.start()
+        copies.append(copy)
+    for copy in copies:
+        copy.wait()
+
+
+def sending(p):
+    rows = pltpu.VMEM((VOX, ROWS, 2 * N), BF16)
+    return [pltpu.VMEM(p.shape, BF16), rows, pltpu.SemaphoreType.DMA((3,))]
 
 
 SCRATCH = [pltpu.VMEM((2, N, N), F32)] * 2 + [pltpu.VMEM((N, N), F32)] * 2
@@ -203,7 +217,7 @@
 
 
 def full_kernel(core_ref, mine_ref, theirs_ref, p_ref, q_ref, r_ref, s_ref, *refs):
-    out_ref, node_hbm, proj_ref, a_ref, c_ref, node_ref, sem = refs[:7]
+    out_ref, node_hbm, proj_hbm, a_ref, c_ref = refs[:5]
     core = core_ref[0]
     for half, ref in ((core, mine_ref), (1 - core, theirs_ref)):
         for y in range(8):
@@ -219,13 +233,9 @@
             c_ref[at, H:] = ref[y, 64:80, :]
     for k in range(2):
         a_ref[k, :H, H:] = a_ref[k, H:, :H].T
-    weights_body(a_ref[0], a_ref[1], c_ref[...], out_ref, *refs[7:])
+    weights_body(a_ref[0], a_ref[1], c_ref[...], out_ref, *refs[8:])
     node = mixed(p_ref, q_ref, out_ref)
-    node_ref[...] = node
-    copy = pltpu.make_async_copy(node_ref, node_hbm, sem)
-    copy.start()
-    project_into(node, (r_ref, s_ref), proj_ref)
-    copy.wait()
+    send_out(node, (r_ref, s_ref), node_hbm, proj_hbm, *refs[5:8])
 
 
 def projections(node):
@@ -238,9 +248,9 @@
         full_kernel,
         out_shape=(WEIGHTS,) + projections(p),
         in_specs=[SMEM] + [VMEM] * 6,
-        out_specs=(VMEM, HBM, VMEM),
+        out_specs=(VMEM, HBM, HBM),
         scratch_shapes=[pltpu.VMEM((2, N, N), F32), pltpu.VMEM((N, N), F32)]
-        + [pltpu.VMEM(p.shape, BF16), pltpu.SemaphoreType.DMA]
+        + sending(p)
         + SCRATCH,
         compiler_params=params(16),
         name="full_merge",
@@ -278,23 +288,23 @@
     )(p, q, w)
 
 
-def project_kernel(p_ref, q_ref, w_ref, r_ref, s_ref, out_hbm, proj_ref, out_ref, sem):
-    out = mixed(p_ref, q_ref, w_ref)
-    out_ref[...] = out
-    copy = pltpu.make_async_copy(out_ref, out_hbm, sem)
+def project_kernel(p_hbm, q_ref, w_ref, r_ref, s_ref, node_hbm, proj_hbm, p_ref, sem, *refs):
+    copy = pltpu.make_async_copy(p_hbm, p_ref, sem)
     copy.start()
-    project_into(out, (r_ref, s_ref), proj_ref)
+    node = dot1(q_ref[...], w_ref[1], NT)
     copy.wait()
+    node = (node + dot1(p_ref[...], w_ref[0], NT)).astype(BF16)
+    send_out(node, (r_ref, s_ref), node_hbm, proj_hbm, *refs)
 
 
 def project(p, q, w, r, s):
     return pl.pallas_call(
         project_kernel,
         out_shape=projections(p),
-        in_specs=[VMEM] * 5,
-        out_specs=(HBM, VMEM),
-        scratch_shapes=[pltpu.VMEM(p.shape, BF16), pltpu.SemaphoreType.DMA],
-        compiler_params=params(8),
+        in_specs=[HBM] + [VMEM] * 4,
+        out_specs=(HBM, HBM),
+        scratch_shapes=[pltpu.VMEM(p.shape, BF16), pltpu.SemaphoreType.DMA] + sending(p),
+        compiler_params=params(10),
         name="project",
     )(p, q, w, r, s)
 
@@ -328,38 +338,38 @@
 
 
 def self_gram_kernel(p_hbm, out_ref, p_ref, sems):
-    half = p_hbm.shape[0] // 2
+    piece = p_hbm.shape[0] // 4
     copies = []
-    for k in range(2):
-        at = pl.ds(half * k, half)
+    for k in range(4):
+        at = pl.ds(piece * k, piece)
         copies.append(pltpu.make_async_copy(p_hbm.at[at], p_ref.at[at], sems.at[k]))
         copies[-1].start()
     total = None
-    for k in range(2):
+    for k in range(4):
         copies[k].wait()
-        at = pl.ds(half * k, half)
+        at = pl.ds(piece * k, piece)
         left, right = p_ref[at, :H], p_ref[at, H:]
         pairs = ((left, left), (right, right), (right, left))
         got = [dot1(a, b, TN) for a, b in pairs]
         total = got if total is None else [x + y for x, y in zip(total, got)]
     for k in range(3):
-        out_ref[:, 8 * k : 8 * k + 8, :] = total[k].reshape(VOX, 8, H)
+        out_ref[:, 8 * k : 8 * k + 8, :] = total[k].astype(BF16).reshape(VOX, 8, H)
 
 
 def self_gram(p):
     return pl.pallas_call(
         self_gram_kernel,
-        out_shape=jax.ShapeDtypeStruct((VOX, 24, H), F32),
+        out_shape=jax.ShapeDtypeStruct((VOX, 24, H), BF16),
         in_specs=[HBM],
         out_specs=VMEM,
-        scratch_shapes=[pltpu.VMEM(p.shape, BF16), pltpu.SemaphoreType.DMA((2,))],
+        scratch_shapes=[pltpu.VMEM(p.shape, BF16), pltpu.SemaphoreType.DMA((4,))],
         compiler_params=params(4),
         name="self_gram",
     )(pltpu.with_memory_space_constraint(p, pltpu.MemorySpace.HBM))
 
 
 def cross_gram_kernel(p_ref, q_ref, out_ref):
-    got = dot1(p_ref[...], q_ref[...], TN)
+    got = dot1(p_ref[...], q_ref[...], TN).astype(BF16)
     out_ref[:, :ROWS, :] = got[:, :H].reshape(VOX, ROWS, H)
     out_ref[:, ROWS:, :] = got[:, H:].reshape(VOX, ROWS, H)
 
@@ -367,7 +377,7 @@
 def cross_gram(p, q):
     return pl.pallas_call(
         cross_gram_kernel,
-        out_shape=jax.ShapeDtypeStruct((VOX, 2 * ROWS, H), F32),
+        out_shape=jax.ShapeDtypeStruct((VOX, 2 * ROWS, H), BF16),
         in_specs=[VMEM, VMEM],
         out_specs=VMEM,
         compiler_params=params(6),

time: 348 us -> 343 us (0.986)
  waiting for transfers between devices: 80.1 us -> 75.1 us
    all_to_all x6, waiting for transfers between devices: 35.4 us -> 31.1 us  [exchange(): return lax.all_to_all(parts, 'vox', 0, 0)]
  transfers between devices with their start and end apart: 16 -> 16, of which waited for: 10 -> 9; matrix products, arithmetic and copies ran while one was open for 0% -> 0% of each run, Pallas kernels for 3% -> 3%
where the time goes in v5:
time: 343 us; the launch traced here: 342 us
  Pallas kernels  180 us (52%)
  waiting for transfers between devices  75.1 us (22%)
  starting transfers between devices  70.5 us (21%)
  blocking collectives  14.3 us (4%)
    pallas_call x1, Pallas kernels, full_merge(): pl.pallas_call(full_kernel, out_shape=(WEIGHTS,) + projections(p), in_spe...  163 us
    ppermute x8, waiting for transfers between devices, partner(): return lax.ppermute(value, 'grp', [(g, g ^ mask) for g in range(GRP)])  36.9 us
    all_to_all x6, starting transfers between devices, exchange(): return lax.all_to_all(parts, 'vox', 0, 0)  36.9 us
    all_to_all x6, waiting for transfers between devices, exchange(): return lax.all_to_all(parts, 'vox', 0, 0)  31.1 us
    ppermute x8, starting transfers between devices, partner(): return lax.ppermute(value, 'grp', [(g, g ^ mask) for g in range(GRP)])  27.7 us
    all_to_all x1, blocking collectives, exchange(): return lax.all_to_all(parts, 'vox', 0, 0)  14.3 us
    all_to_all x1, waiting for transfers between devices, same_core(): return lax.all_to_all(sent, 'vox', 0, 0, axis_index_groups=groups)  7.07 us
  transfers between devices with their start and end apart: 16, of which 9 were waited for; matrix products, arithmetic and copies ran while one was open for 0% of the time, Pallas kernels for 3%

profile of v5, /device:TPU:1, one launch (start us, length us, event | category | flops | bytes accessed | tf_op | source)
XLA Modules:
  0.0 342.2 jit_solution(12803776662430120110)
XLA Ops:
  0.0 4.1 %collective-permute-start.1 = (bf16[1024,256]{1,0:T(8,128)(2,1)}, bf16[1024,256]{1,0:T(8,128)(2,1)S(1)}, u32[]{:S(2)}, u32[]{:S(2)}) collective-permute-start(bf16[1024,256]{1,0:T(8,128)(2,1)} %bitcast.6), channel_id=1, source_target_pairs={{0,16},{16,0},{32,48},{48,32},{64,80},{80,64},{96,112},{112,96},{1... | collective-permute-start | bytes 1572872 | tf_op jit(solution)/shard_map/ppermute | solution.py:410
  4.1 2.4 self_gram.1
  6.5 8.1 %all-to-all-start = ((bf16[16,24,128]{2,1,0:T(8,128)(2,1)}), bf16[16,24,128]{2,1,0:T(8,128)(2,1)S(1)}, u32[]{:S(2)}, u32[]{:S(2)}) async-start(bf16[16,24,128]{2,1,0:T(8,128)(2,1)} %self_gram.1), calls=%async_computation | async-start | bytes 196608 | tf_op jit(solution)/shard_map/all_to_all | solution.py:414
  14.6 0.0 collective-permute-done.1.q_ref
  14.6 0.0 copy-done
  14.6 1.0 cross_gram.1
  15.7 7.5 %all-to-all-done = bf16[16,24,128]{2,1,0:T(8,128)(2,1)S(1)} async-done(((bf16[16,24,128]{2,1,0:T(8,128)(2,1)}), bf16[16,24,128]{2,1,0:T(8,128)(2,1)S(1)}, u32[]{:S(2)}, u32[]{:S(2)}) %all-to-all-start) | async-done | bytes 98336 | tf_op jit(solution)/shard_map/all_to_all | solution.py:414
  23.1 3.4 all-to-all-start.1
  26.6 3.6 %collective-permute-start = (f32[24,128]{1,0:T(8,128)S(1)}, f32[24,128]{1,0:T(8,128)S(1)}, u32[]{:S(2)}, u32[]{:S(2)}) collective-permute-start(f32[24,128]{1,0:T(8,128)S(1)} %convert_reduce_fusion.2), channel_id=1, source_target_pairs={{0,16},{16,0},{32,48},{48,32},{64,80},{80,64},{96,112},{112,96},{1... | collective-permute-start | bytes 36872 | tf_op jit(solution)/shard_map/ppermute | solution.py:410
  30.2 5.0 %all-to-all-done.1 = bf16[16,32,128]{2,1,0:T(8,128)(2,1)S(1)} async-done(((bf16[16,32,128]{2,1,0:T(8,128)(2,1)}), bf16[16,32,128]{2,1,0:T(8,128)(2,1)S(1)}, u32[]{:S(2)}, u32[]{:S(2)}) %all-to-all-start.1) | async-done | bytes 131104 | tf_op jit(solution)/shard_map/all_to_all | solution.py:414
  35.2 0.0 collective-permute-done
  35.3 0.7 broadcast_in_dim.4
  36.0 3.4 %all-to-all-start.2 = ((f32[8,80,128]{2,1,0:T(8,128)}), f32[8,80,128]{2,1,0:T(8,128)S(1)}, u32[]{:S(2)}, u32[]{:S(2)}) async-start(f32[8,80,128]{2,1,0:T(8,128)} %broadcast_in_dim.4), calls=%async_computation.2 | async-start | bytes 655360 | tf_op jit(solution)/shard_map/all_to_all | solution.py:420
  39.5 3.7 %collective-permute-start.3 = (bf16[1024,256]{1,0:T(8,128)(2,1)S(1)}, bf16[1024,256]{1,0:T(8,128)(2,1)S(1)}, u32[]{:S(2)}, u32[]{:S(2)}) collective-permute-start(bf16[1024,256]{1,0:T(8,128)(2,1)S(1)} %bitcast.9), channel_id=1, source_target_pairs={{0,48},{16,32},{32,16},{48,0},{64,112},{80,96},{96,80},{112,64},{1... | collective-permute-start | bytes 1572872 | tf_op jit(solution)/shard_map/ppermute | solution.py:410
  43.1 2.8 collective-permute-start.4
  46.0 7.1 %all-to-all-done.2.mine_ref = f32[8,80,128]{2,1,0:T(8,128)S(1)} async-done(((f32[8,80,128]{2,1,0:T(8,128)}), f32[8,80,128]{2,1,0:T(8,128)S(1)}, u32[]{:S(2)}, u32[]{:S(2)}) %all-to-all-start.2) | async-done | bytes 327712 | tf_op jit(solution)/shard_map/all_to_all | solution.py:420
  53.0 2.5 collective-permute-start.2
  55.5 0.0 collective-permute-done.3.r_ref.p_ref
  55.5 11.2 %collective-permute-done.4.s_ref.q_ref = bf16[1024,256]{1,0:T(8,128)(2,1)S(1)} collective-permute-done((bf16[1024,256]{1,0:T(8,128)(2,1)S(1)}, bf16[1024,256]{1,0:T(8,128)(2,1)S(1)}, u32[]{:S(2)}, u32[]{:S(2)}) %collective-permute-start.4) | collective-permute-done | bytes 524320 | tf_op jit(solution)/shard_map/ppermute | solution.py:410
  66.7 0.0 collective-permute-done.2.theirs_ref
  66.7 162.7 %full_merge.1 = (bf16[2,256,256]{2,1,0:T(8,128)(2,1)S(1)}, bf16[1024,256]{1,0:T(8,128)(2,1)S(1)}, bf16[16,16,512]{2,1,0:T(8,128)(2,1)}) custom-call(s32[1]{0:T(128)} %bitcast.core_ref, f32[8,80,128]{2,1,0:T(8,128)S(1)} %all-to-all-done.2.mine_ref, f32[8,80,128]{2,1,0:T(8,128)S(1)} %collective-permute-done.2.theirs_ref, bf16[1024,256]{1,0:T(8,128)(2,1)S(1)} %bitcast.10, ...), custom_call_target="tpu_custom_call" | custom-call | tf_op jit(solution)/shard_map/full_merge/pallas_call | solution.py:247
  229.5 0.0 copy-start.1
  229.5 0.7 copy-done.1
  230.2 8.2 %all-to-all-start.3 = ((bf16[16,16,512]{2,1,0:T(8,128)(2,1)}), bf16[16,16,512]{2,1,0:T(8,128)(2,1)S(1)}, u32[]{:S(2)}, u32[]{:S(2)}) async-start(bf16[16,16,512]{2,1,0:T(8,128)(2,1)} %get-tuple-element.12), calls=%async_computation.3 | async-start | bytes 524288 | tf_op jit(solution)/shard_map/all_to_all | solution.py:414
  238.4 3.9 %collective-permute-start.6 = (bf16[1024,256]{1,0:T(8,128)(2,1)S(1)}, bf16[1024,256]{1,0:T(8,128)(2,1)S(1)}, u32[]{:S(2)}, u32[]{:S(2)}) collective-permute-start(bf16[1024,256]{1,0:T(8,128)(2,1)S(1)} %get-tuple-element.10.p_hbm), channel_id=1, source_target_pairs={{0,64},{16,80},{32,96},{48,112},{64,0},{80,16},{96,32},{112,48},{1... | collective-permute-start | bytes 1572872 | tf_op jit(solution)/shard_map/ppermute | solution.py:410
  242.3 3.5 %collective-permute-start.7 = (bf16[1024,256]{1,0:T(8,128)(2,1)S(1)}, bf16[1024,256]{1,0:T(8,128)(2,1)S(1)}, u32[]{:S(2)}, u32[]{:S(2)}) collective-permute-start(bf16[1024,256]{1,0:T(8,128)(2,1)S(1)} %get-tuple-element.10.p_hbm), channel_id=1, source_target_pairs={{0,112},{16,96},{32,80},{48,64},{64,48},{80,32},{96,16},{112,0},{1... | collective-permute-start | bytes 1572872 | tf_op jit(solution)/shard_map/ppermute | solution.py:410
  245.8 2.8 collective-permute-start.5
  248.6 19.2 %collective-permute-done.5.w_ref = bf16[2,256,256]{2,1,0:T(8,128)(2,1)S(1)} collective-permute-done((bf16[2,256,256]{2,1,0:T(8,128)(2,1)}, bf16[2,256,256]{2,1,0:T(8,128)(2,1)S(1)}, u32[]{:S(2)}, u32[]{:S(2)}) %collective-permute-start.5) | collective-permute-done | bytes 262176 | tf_op jit(solution)/shard_map/ppermute | solution.py:410
  267.8 0.0 all-to-all-done.3.parts_ref
  267.8 0.9 cross_rows.2
  268.7 8.1 %all-to-all-start.4 = ((bf16[16,16,256]{2,1,0:T(8,128)(2,1)}), bf16[16,16,256]{2,1,0:T(8,128)(2,1)S(1)}, u32[]{:S(2)}, u32[]{:S(2)}) async-start(bf16[16,16,256]{2,1,0:T(8,128)(2,1)} %cross_rows.2), calls=%async_computation.4 | async-start | bytes 262144 | tf_op jit(solution)/shard_map/all_to_all | solution.py:414
  276.8 0.5 mix.2.q_ref
  277.3 8.4 %all-to-all-done.4 = bf16[16,16,256]{2,1,0:T(8,128)(2,1)S(1)} async-done(((bf16[16,16,256]{2,1,0:T(8,128)(2,1)}), bf16[16,16,256]{2,1,0:T(8,128)(2,1)S(1)}, u32[]{:S(2)}, u32[]{:S(2)}) %all-to-all-start.4) | async-done | bytes 131104 | tf_op jit(solution)/shard_map/all_to_all | solution.py:414
  285.7 3.7 %plain_weights.1.w_ref = bf16[2,256,256]{2,1,0:T(8,128)(2,1)S(1)} custom-call(bf16[256,256]{1,0:T(8,128)(2,1)S(1)} %bitcast.12), custom_call_target="tpu_custom_call" | custom-call | tf_op jit(solution)/shard_map/plain_weights/pallas_call | solution.py:265
  289.4 0.0 collective-permute-done.6.r_ref.p_ref
  289.4 0.0 collective-permute-done.7.s_ref.q_ref
  289.4 2.2 project.1
  291.7 3.4 %all-to-all-start.5 = ((bf16[16,16,512]{2,1,0:T(8,128)(2,1)}), bf16[16,16,512]{2,1,0:T(8,128)(2,1)S(1)}, u32[]{:S(2)}, u32[]{:S(2)}) async-start(bf16[16,16,512]{2,1,0:T(8,128)(2,1)} %get-tuple-element.13), calls=%async_computation.5 | async-start | bytes 524288 | tf_op jit(solution)/shard_map/all_to_all | solution.py:414
  295.1 3.4 collective-permute-start.8
  298.5 6.4 %collective-permute-done.8.w_ref = bf16[2,256,256]{2,1,0:T(8,128)(2,1)S(1)} collective-permute-done((bf16[2,256,256]{2,1,0:T(8,128)(2,1)S(1)}, bf16[2,256,256]{2,1,0:T(8,128)(2,1)S(1)}, u32[]{:S(2)}, u32[]{:S(2)}) %collective-permute-start.8) | collective-permute-done | bytes 262176 | tf_op jit(solution)/shard_map/ppermute | solution.py:410
  304.9 1.9 all-to-all-done.5.parts_ref
  306.8 0.9 cross_rows.3
  307.7 5.6 %all-to-all-start.6 = ((bf16[16,16,256]{2,1,0:T(8,128)(2,1)}), bf16[16,16,256]{2,1,0:T(8,128)(2,1)S(1)}, u32[]{:S(2)}, u32[]{:S(2)}) async-start(bf16[16,16,256]{2,1,0:T(8,128)(2,1)} %cross_rows.3), calls=%async_computation.6 | async-start | bytes 262144 | tf_op jit(solution)/shard_map/all_to_all | solution.py:414
  313.3 0.5 mix.3.q_ref
  313.8 8.4 %all-to-all-done.6 = bf16[16,16,256]{2,1,0:T(8,128)(2,1)S(1)} async-done(((bf16[16,16,256]{2,1,0:T(8,128)(2,1)}), bf16[16,16,256]{2,1,0:T(8,128)(2,1)S(1)}, u32[]{:S(2)}, u32[]{:S(2)}) %all-to-all-start.6) | async-done | bytes 131104 | tf_op jit(solution)/shard_map/all_to_all | solution.py:414
  322.2 5.2 %last_merge.1 = bf16[16,16,512]{2,1,0:T(8,128)(2,1)S(1)} custom-call(bf16[256,256]{1,0:T(8,128)(2,1)S(1)} %bitcast.11, bf16[1024,256]{1,0:T(8,128)(2,1)S(1)} %get-tuple-element.14.p_hbm, bf16[1024,256]{1,0:T(8,128)(2,1)S(1)} %mix.3.q_ref, bf16[1024,512]{1,0:T(8,128)(2,1)} %bitcast.13), custom_call_target="tpu_custom_call" | custom-call | tf_op jit(solution)/shard_map/last_merge/pallas_call | solution.py:326
  327.3 14.3 %all_to_all.40 = bf16[16,16,512]{2,1,0:T(8,128)(2,1)S(1)} all-to-all(bf16[16,16,512]{2,1,0:T(8,128)(2,1)S(1)} %last_merge.1), channel_id=1, replica_groups=mesh['grp'=32,'vox'=16] {'vox'}, dimensions={0} | all-to-all | bytes 524288 | tf_op jit(solution)/shard_map/all_to_all | solution.py:414
  341.6 0.7 convert_reduce_fusion
  (4 shorter events, 0.1 us)
Async XLA Ops:
  0.0 14.6 %copy-start = (bf16[1,1024,256]{2,1,0:T(8,128)(2,1)S(1)}, bf16[1,1024,256]{2,1,0:T(8,128)(2,1)}, u32[]{:S(2)}) copy-start(bf16[1,1024,256]{2,1,0:T(8,128)(2,1)} %param.2) | copy-start | bytes 1572868
  0.0 14.6 %collective-permute-start.1 = (bf16[1024,256]{1,0:T(8,128)(2,1)}, bf16[1024,256]{1,0:T(8,128)(2,1)S(1)}, u32[]{:S(2)}, u32[]{:S(2)}) collective-permute-start(bf16[1024,256]{1,0:T(8,128)(2,1)} %bitcast.6), channel_id=1, source_target_pairs={{0,16},{16,0},{32,48},{48,32},{64,80},{80,64},{96,112},{112,96},{1... | collective-permute-start | bytes 1572872 | tf_op jit(solution)/shard_map/ppermute | solution.py:410
  6.5 16.6 %all-to-all-start = ((bf16[16,24,128]{2,1,0:T(8,128)(2,1)}), bf16[16,24,128]{2,1,0:T(8,128)(2,1)S(1)}, u32[]{:S(2)}, u32[]{:S(2)}) async-start(bf16[16,24,128]{2,1,0:T(8,128)(2,1)} %self_gram.1), calls=%async_computation | async-start | bytes 196608 | tf_op jit(solution)/shard_map/all_to_all | solution.py:414
  23.1 12.1 %all-to-all-start.1 = ((bf16[16,32,128]{2,1,0:T(8,128)(2,1)}), bf16[16,32,128]{2,1,0:T(8,128)(2,1)S(1)}, u32[]{:S(2)}, u32[]{:S(2)}) async-start(bf16[16,32,128]{2,1,0:T(8,128)(2,1)} %cross_gram.1), calls=%async_computation.1 | async-start | bytes 262144 | tf_op jit(solution)/shard_map/all_to_all | solution.py:414
  26.6 8.7 %collective-permute-start = (f32[24,128]{1,0:T(8,128)S(1)}, f32[24,128]{1,0:T(8,128)S(1)}, u32[]{:S(2)}, u32[]{:S(2)}) collective-permute-start(f32[24,128]{1,0:T(8,128)S(1)} %convert_reduce_fusion.2), channel_id=1, source_target_pairs={{0,16},{16,0},{32,48},{48,32},{64,80},{80,64},{96,112},{112,96},{1... | collective-permute-start | bytes 36872 | tf_op jit(solution)/shard_map/ppermute | solution.py:410
  36.0 17.0 %all-to-all-start.2 = ((f32[8,80,128]{2,1,0:T(8,128)}), f32[8,80,128]{2,1,0:T(8,128)S(1)}, u32[]{:S(2)}, u32[]{:S(2)}) async-start(f32[8,80,128]{2,1,0:T(8,128)} %broadcast_in_dim.4), calls=%async_computation.2 | async-start | bytes 655360 | tf_op jit(solution)/shard_map/all_to_all | solution.py:420
  39.5 16.1 %collective-permute-start.3 = (bf16[1024,256]{1,0:T(8,128)(2,1)S(1)}, bf16[1024,256]{1,0:T(8,128)(2,1)S(1)}, u32[]{:S(2)}, u32[]{:S(2)}) collective-permute-start(bf16[1024,256]{1,0:T(8,128)(2,1)S(1)} %bitcast.9), channel_id=1, source_target_pairs={{0,48},{16,32},{32,16},{48,0},{64,112},{80,96},{96,80},{112,64},{1... | collective-permute-start | bytes 1572872 | tf_op jit(solution)/shard_map/ppermute | solution.py:410
  43.1 23.6 %collective-permute-start.4 = (bf16[1024,256]{1,0:T(8,128)(2,1)S(1)}, bf16[1024,256]{1,0:T(8,128)(2,1)S(1)}, u32[]{:S(2)}, u32[]{:S(2)}) collective-permute-start(bf16[1024,256]{1,0:T(8,128)(2,1)S(1)} %collective-permute-done.1.q_ref), channel_id=1, source_target_pairs={{0,48},{16,32},{32,16},{48,0},{64,112},{80,96},{96,80},{112,64},{1... | collective-permute-start | bytes 1572872 | tf_op jit(solution)/shard_map/ppermute | solution.py:410
  53.0 13.7 %collective-permute-start.2 = (f32[8,80,128]{2,1,0:T(8,128)S(1)}, f32[8,80,128]{2,1,0:T(8,128)S(1)}, u32[]{:S(2)}, u32[]{:S(2)}) collective-permute-start(f32[8,80,128]{2,1,0:T(8,128)S(1)} %all-to-all-done.2.mine_ref), channel_id=1, source_target_pairs={{0,1},{1,0},{2,3},{3,2},{4,5},{5,4},{6,7},{7,6},{8,9},{9,8},{10,11... | collective-permute-start | bytes 983048 | tf_op jit(solution)/shard_map/ppermute | solution.py:424
  229.5 0.7 copy-start.1
  230.2 37.6 %all-to-all-start.3 = ((bf16[16,16,512]{2,1,0:T(8,128)(2,1)}), bf16[16,16,512]{2,1,0:T(8,128)(2,1)S(1)}, u32[]{:S(2)}, u32[]{:S(2)}) async-start(bf16[16,16,512]{2,1,0:T(8,128)(2,1)} %get-tuple-element.12), calls=%async_computation.3 | async-start | bytes 524288 | tf_op jit(solution)/shard_map/all_to_all | solution.py:414
  238.4 51.0 %collective-permute-start.6 = (bf16[1024,256]{1,0:T(8,128)(2,1)S(1)}, bf16[1024,256]{1,0:T(8,128)(2,1)S(1)}, u32[]{:S(2)}, u32[]{:S(2)}) collective-permute-start(bf16[1024,256]{1,0:T(8,128)(2,1)S(1)} %get-tuple-element.10.p_hbm), channel_id=1, source_target_pairs={{0,64},{16,80},{32,96},{48,112},{64,0},{80,16},{96,32},{112,48},{1... | collective-permute-start | bytes 1572872 | tf_op jit(solution)/shard_map/ppermute | solution.py:410
  242.3 47.1 %collective-permute-start.7 = (bf16[1024,256]{1,0:T(8,128)(2,1)S(1)}, bf16[1024,256]{1,0:T(8,128)(2,1)S(1)}, u32[]{:S(2)}, u32[]{:S(2)}) collective-permute-start(bf16[1024,256]{1,0:T(8,128)(2,1)S(1)} %get-tuple-element.10.p_hbm), channel_id=1, source_target_pairs={{0,112},{16,96},{32,80},{48,64},{64,48},{80,32},{96,16},{112,0},{1... | collective-permute-start | bytes 1572872 | tf_op jit(solution)/shard_map/ppermute | solution.py:410
  245.8 22.0 %collective-permute-start.5 = (bf16[2,256,256]{2,1,0:T(8,128)(2,1)}, bf16[2,256,256]{2,1,0:T(8,128)(2,1)S(1)}, u32[]{:S(2)}, u32[]{:S(2)}) collective-permute-start(bf16[2,256,256]{2,1,0:T(8,128)(2,1)} %copy-done.1), channel_id=1, source_target_pairs={{0,48},{16,32},{32,16},{48,0},{64,112},{80,96},{96,80},{112,64},{1... | collective-permute-start | bytes 786440 | tf_op jit(solution)/shard_map/ppermute | solution.py:410
  268.7 17.0 %all-to-all-start.4 = ((bf16[16,16,256]{2,1,0:T(8,128)(2,1)}), bf16[16,16,256]{2,1,0:T(8,128)(2,1)S(1)}, u32[]{:S(2)}, u32[]{:S(2)}) async-start(bf16[16,16,256]{2,1,0:T(8,128)(2,1)} %cross_rows.2), calls=%async_computation.4 | async-start | bytes 262144 | tf_op jit(solution)/shard_map/all_to_all | solution.py:414
  291.7 15.1 %all-to-all-start.5 = ((bf16[16,16,512]{2,1,0:T(8,128)(2,1)}), bf16[16,16,512]{2,1,0:T(8,128)(2,1)S(1)}, u32[]{:S(2)}, u32[]{:S(2)}) async-start(bf16[16,16,512]{2,1,0:T(8,128)(2,1)} %get-tuple-element.13), calls=%async_computation.5 | async-start | bytes 524288 | tf_op jit(solution)/shard_map/all_to_all | solution.py:414
  295.1 9.8 %collective-permute-start.8 = (bf16[2,256,256]{2,1,0:T(8,128)(2,1)S(1)}, bf16[2,256,256]{2,1,0:T(8,128)(2,1)S(1)}, u32[]{:S(2)}, u32[]{:S(2)}) collective-permute-start(bf16[2,256,256]{2,1,0:T(8,128)(2,1)S(1)} %plain_weights.1.w_ref), channel_id=1, source_target_pairs={{0,64},{16,80},{32,96},{48,112},{64,0},{80,16},{96,32},{112,48},{1... | collective-permute-start | bytes 786440 | tf_op jit(solution)/shard_map/ppermute | solution.py:410
  307.7 14.5 %all-to-all-start.6 = ((bf16[16,16,256]{2,1,0:T(8,128)(2,1)}), bf16[16,16,256]{2,1,0:T(8,128)(2,1)S(1)}, u32[]{:S(2)}, u32[]{:S(2)}) async-start(bf16[16,16,256]{2,1,0:T(8,128)(2,1)} %cross_rows.3), calls=%async_computation.6 | async-start | bytes 262144 | tf_op jit(solution)/shard_map/all_to_all | solution.py:414
